TPU v7x, 32 devices: a whole 2x2x4 slice. The times are simulated.
32 devices in a mesh: node: 8 (over z, x), query: 4 (over y, core).
Axes of the slice: x: 2, y: 2, z: 4, core: 2. Of those that a mesh axis runs over, the one named last changes fastest.
Arguments:
- entity_state: bfloat16 [8192, 2048], P('node', 'query'), may hold values from -6 to 6
- edge_tiles: int32 [128, 3, 512], P('node'), may hold values from 0 to 4095, as said below
- query_head: int32 [64], P('query'), may hold values from 0 to 8191
- query_relation: int32 [64], P('query'), may hold values from 0 to 821
- query_table: float32 [822, 32], replicated, may hold values from -6 to 6
- rel_vectors: float32 [2, 822, 32], replicated, may hold values from -1.8 to 1.8
- mix_weight: float32 [2, 32, 32], replicated, may hold values from -1 to 1
- mix_bias: float32 [2, 32], replicated, may hold values from -3 to 3
- cotangent: bfloat16 [8192, 2048], P('node', 'query'), may hold values from -6 to 6
Outputs:
- final_state: bfloat16 [8192, 2048], P('node', 'query')
- weight_grads: float32 [2, 32, 32], replicated
- bias_grads: float32 [2, 32], replicated
Inputs may be any that keep to these rules, and one draw needn't show every extreme that they name: edge_tiles[t,0,:] lies in 0 to 4095, edge_tiles[t,1,:] in 0 to 63, edge_tiles[t,2,:] in 0 to 821.
All inputs are finite; a program needn't handle non-finite values.
Results may differ from a plain program's by a relative error of at most 0.0056.
Values may be sent and summed in bfloat16 or wider, within the bound.
No kernel may reach another device: no remote copies, remote signals or barrier semaphores. Data moves between devices by JAX's collectives and lax.ppermute only.
A program may use at most 192 MiB of HBM per device.

v0:
```python
import functools

import jax
import jax.numpy as jnp
from jax import lax
from jax.experimental import pallas as pl
from jax.experimental.pallas import tpu as pltpu
from jax.sharding import PartitionSpec as P


DIM = 32
LANES = 128
UNROLL = 48
SUMS = 3
CHUNK = 256
DENSE = 512
LINE = 1024
AXES = ("node", "query")
HIGHEST = lax.Precision.HIGHEST
SMEM = pl.BlockSpec(memory_space=pltpu.SMEM)
VMEM = pl.BlockSpec(memory_space=pltpu.VMEM)
ANY = pl.BlockSpec(memory_space=pl.ANY)


def silu_slope(values):
    sigma = jax.nn.sigmoid(values)
    return sigma * (1.0 + values * (1.0 - sigma))


class Seats:
    def __init__(self, nodes, queries):
        self.nodes, self.queries = nodes, queries

    def home(self, part, column):
        return part * self.queries + column

    def seat(self, part, column):
        half = self.nodes // 2
        low = part % half
        node = (column & 1) * half + (low ^ (low >> 1))
        return node * self.queries + (column >> 1) * 2 + part // half

    def blocks(self):
        return [(p, c) for p in range(self.nodes) for c in range(self.queries)]

    def gather(self):
        return [(self.home(p, c), self.seat(p, c)) for p, c in self.blocks()]

    def give_back(self):
        return [(target, source) for source, target in self.gather()]

    def shift(self, step):
        return [
            (self.seat((p - step) % self.nodes, c), self.seat(p, c)) for p, c in self.blocks()
        ]

    def mirror(self):
        return [
            (self.seat(p, c), self.seat((p + self.nodes // 2) % self.nodes, c))
            for p, c in self.blocks()
        ]

    def parts(self):
        table = [0] * (self.nodes * self.queries)
        for p, c in self.blocks():
            table[self.seat(p, c)] = p
        return table


def spread(block_ref, window_ref, first):
    if block_ref.shape[1] == LANES:
        rows = block_ref.shape[0]

        def step(i, carry):
            at = pl.multiple_of(i * CHUNK, CHUNK)
            window_ref[pl.ds(first + at, CHUNK), :] = block_ref[pl.ds(at, CHUNK), :].astype(
                jnp.float32
            )
            return carry

        lax.fori_loop(0, rows // CHUNK, step, 0)
        return
    rows, cols = block_ref.shape
    groups = cols // LANES
    size = CHUNK // groups

    def step(i, carry):
        at = pl.multiple_of(i * size, size)
        for j in range(groups):
            window_ref[pl.ds(first + at * groups + j, size, stride=groups), :] = block_ref[
                pl.ds(at, size), j * LANES : (j + 1) * LANES
            ].astype(jnp.float32)
        return carry

    lax.fori_loop(0, rows // size, step, 0)


def clear(sums):
    def step(i, carry):
        at = pl.multiple_of(i * CHUNK, CHUNK)
        for ref in sums:
            ref[pl.ds(at, CHUNK), :] = jnp.zeros((CHUNK, LANES), jnp.float32)
        return carry

    lax.fori_loop(0, sums[0].shape[0] // CHUNK, step, 0)


def walk(groups, begin, end, from_ref, to_ref, rel_ref, window, table, sums):
    room = from_ref.shape[0] - UNROLL
    views = [[ref.at[pl.ds(u, room)] for ref in (from_ref, to_ref, rel_ref)] for u in range(UNROLL)]

    def step(i, carry):
        first = begin + i * UNROLL
        for u, (from_view, to_view, rel_view) in enumerate(views):
            source = pl.multiple_of(from_view[first], groups)
            target = pl.multiple_of(to_view[first], groups)
            scale = table[pl.ds(rel_view[first], groups, stride=0), :]
            sums[u % SUMS][pl.ds(target, groups), :] += (
                window[pl.ds(source, groups), :] * scale
            )
        return carry

    lax.fori_loop(0, (end - begin) // UNROLL, step, 0)


def total_of(sums, at, size=CHUNK):
    value = sums[0][pl.ds(at, size), :]
    for ref in sums[1:]:
        value = value + ref[pl.ds(at, size), :]
    return value


def fetch(pairs, sems):
    copies = [pltpu.make_async_copy(src, dst, sems.at[i]) for i, (src, dst) in enumerate(pairs)]
    for copy in copies:
        copy.start()
    return copies


def wait(copies):
    for copy in copies:
        copy.wait()


def bucket_kernel(
    edges_ref, out_ref, ends_ref, slots, rows, rels, pos, word, meta, pos_buf, word_buf, meta_buf,
    sems, *, tile_count, row_count, rel_count,
):
    lines = slots.shape[0]
    first = 64 * lax.broadcasted_iota(jnp.int32, (tile_count, LANES), 0)
    for j in range(lines // tile_count):
        piece = slice(j * tile_count, (j + 1) * tile_count)
        lanes = slice(j * LANES, (j + 1) * LANES)
        slots[piece, :] = edges_ref[0, :, lanes]
        rows[piece, :] = edges_ref[1, :, lanes] + first
        rels[piece, :] = edges_ref[2, :, lanes]
    slot = slots[...]
    quarter = sum(((slot >= k * row_count).astype(jnp.int32) for k in range(1, 4)))
    local = slot - quarter * row_count
    kind = jnp.where(
        quarter == 1, 0, jnp.where(quarter == 3, 1, jnp.where(quarter == 0, 2, 3))
    )
    second = jnp.where((kind == 1) | (kind == 3), row_count, 0)
    row_bits = (row_count - 1).bit_length()
    word[...] = (rels[...] << (2 * row_bits + 1)) | (rows[...] << (row_bits + 1)) | (second + local)
    shape = (LANES, LANES)
    upto = (lax.broadcasted_iota(jnp.int32, shape, 0) <= lax.broadcasted_iota(jnp.int32, shape, 1))
    upto = upto.astype(jnp.float32).astype(jnp.bfloat16)
    shape = (lines, lines)
    above = (lax.broadcasted_iota(jnp.int32, shape, 0) > lax.broadcasted_iota(jnp.int32, shape, 1))
    above = above.astype(jnp.float32).astype(jnp.bfloat16)
    ones = jnp.ones((LANES, LANES), jnp.bfloat16)
    place = jnp.zeros((lines, LANES), jnp.float32)
    begin = jnp.zeros((1, LANES), jnp.float32)
    for k in range(4):
        chosen = (kind == k).astype(jnp.float32)
        onehot = chosen.astype(jnp.bfloat16)
        within = jnp.dot(onehot, upto, preferred_element_type=jnp.float32)
        per_line = jnp.dot(onehot, ones, preferred_element_type=jnp.float32)
        before = jnp.dot(above, per_line.astype(jnp.bfloat16), preferred_element_type=jnp.float32)
        count = jnp.sum(per_line, axis=0, keepdims=True)
        place = place + chosen * (begin + before + within - 1.0)
        meta[k : k + 1, :] = (begin + count).astype(jnp.int32)
        begin = begin + jnp.floor((count + (UNROLL - 0.5)) / UNROLL) * UNROLL
        meta[k + 4 : k + 5, :] = begin.astype(jnp.int32)
    pos[...] = place.astype(jnp.int32)
    wait(fetch([(pos, pos_buf), (word, word_buf), (meta, meta_buf)], sems))

    def step(i, carry):
        for u in range(LANES):
            out_ref[pos_buf[i, u]] = word_buf[i, u]
        return carry

    lax.fori_loop(0, lines, step, 0)
    dummy = rel_count << (2 * row_bits + 1)

    def fill(i, carry):
        out_ref[i] = dummy
        return carry

    for k in range(4):
        lax.fori_loop(meta_buf[k, 0], meta_buf[k + 4, 0], fill, 0)
        ends_ref[k] = meta_buf[k + 4, 0]


def split(values):
    high = values.astype(jnp.bfloat16)
    low = (values - high.astype(jnp.float32)).astype(jnp.bfloat16)
    return jnp.concatenate([high, low], axis=1)


def split_weight(weight):
    wide = split(weight)
    return jnp.concatenate([wide, wide], axis=0)


def times(values, wide):
    both = jnp.dot(split(values), wide, preferred_element_type=jnp.float32)
    return both[:, :LANES] + both[:, LANES:]


def outer(left, right):
    return lax.dot_general(
        split(left), split(right), (((0,), (0,)), ((), ())), preferred_element_type=jnp.float32
    )


def quarters(wide):
    return (
        wide[:LANES, :LANES] + wide[LANES:, :LANES] + wide[:LANES, LANES:] + wide[LANES:, LANES:]
    )


def near_kernel(
    groups, index, flat, own, mirror, tables, out,
    source, target, rel, tail, own_buf, mirror_buf, table_buf, window, sems, *sums,
):
    long = sums[0].shape[0]
    lists = fetch_lists(flat, (source, target, rel, tail), tables, index, table_buf, sems)
    states = fetch([(own, own_buf), (mirror, mirror_buf)], sems.at[pl.ds(5, 2)])
    clear(sums)
    states[0].wait()
    spread(own_buf, window, 0)
    states[1].wait()
    spread(mirror_buf, window, long)
    wait(lists)
    walk(groups, 0, tail[1], source, target, rel, window, table_buf, sums)
    parts = 4
    size = long // parts
    stores = []
    for k in range(parts):

        def step(i, carry):
            at = pl.multiple_of(k * size + i * CHUNK, CHUNK)
            sums[0][pl.ds(at, CHUNK), :] = total_of(sums, at)
            return carry

        lax.fori_loop(0, size // CHUNK, step, 0)
        piece = pl.ds(k * size, size)
        stores += fetch([(sums[0].at[piece, :], out.at[piece, :])], sems.at[pl.ds(7 + k, 1)])
    wait(stores)


def add_boundary(groups, heads, head_rows, ref, long):
    for q in range(head_rows.shape[0]):
        row = heads[4 + q]

        @pl.when((row >= 0) & (row < long // groups))
        def _():
            at = row * groups + q * DIM // LANES
            ref[pl.ds(at, 1), :] += head_rows[q : q + 1, :]


def fetch_lists(flat, bufs, tables, index, table_buf, sems):
    room = bufs[0].shape[0]
    pairs = [(flat.at[pl.ds(k * room, buf.shape[0])], buf) for k, buf in enumerate(bufs)]
    return fetch(pairs + [(tables.at[index], table_buf)], sems)


def far_sums(groups, long, index, flat, tables, states, list_bufs, bufs, head_rows, window, sems, sums):
    left, right, near = states
    left_buf, right_buf, table_buf = bufs
    lists = fetch_lists(flat, list_bufs, tables, index, table_buf, sems)
    states = fetch(
        [(left, left_buf), (right, right_buf), (near, sums[0].at[pl.ds(0, long), :])],
        sems.at[pl.ds(5, 3)],
    )
    clear([ref.at[pl.ds(0, long), :] for ref in sums[1:]])
    states[0].wait()
    spread(left_buf, window, 0)
    states[1].wait()
    spread(right_buf, window, long)
    states[2].wait()
    wait(lists)
    _, _, _, tail = list_bufs
    add_boundary(groups, tail, head_rows, sums[0], long)


def first_kernel(
    groups, head_rows, weights, biases, flat, left, right, near, tables, own, state, mixed, update,
    source, target, rel, tail, left_buf, right_buf, table_buf, own_buf, window, mixed_buf, update_buf,
    state_buf, sems, *sums,
):
    long = sums[0].shape[0]
    far_sums(
        groups, long, 0, flat, tables, (left, right, near), (source, target, rel, tail),
        (left_buf, right_buf, table_buf), head_rows, window, sems, sums,
    )
    extra = fetch([(own, own_buf)], sems.at[pl.ds(8, 1)])
    walk(groups, tail[1], tail[3], source, target, rel, window, table_buf, sums)
    wait(extra)
    spread(own_buf, window, 0)
    wide = split_weight(weights[0])
    bias = biases[0]
    parts = 4
    size = long // parts
    stores = []
    for k in range(parts):

        def step(i, carry):
            at = pl.multiple_of(k * size + i * DENSE, DENSE)
            rows = pl.ds(at, DENSE)
            mix = total_of(sums, at, DENSE)
            values = times(mix, wide) + bias
            mixed_buf[rows, :] = mix
            update_buf[rows, :] = values
            state_buf[rows, :] = (window[rows, :] + values * jax.nn.sigmoid(values)).astype(
                jnp.bfloat16
            )
            return carry

        lax.fori_loop(0, size // DENSE, step, 0)
        rows = pl.ds(k * size, size)
        stores += fetch(
            [
                (state_buf.at[rows, :], state.at[rows, :]),
                (mixed_buf.at[rows, :], mixed.at[rows, :]),
                (update_buf.at[rows, :], update.at[rows, :]),
            ],
            sems.at[pl.ds(9 + 3 * k, 3)],
        )
    wait(stores)


def second_kernel(
    groups, head_rows, weights, biases, flat, left, right, near, tables, own, cotangent,
    state, grad_mixed, mixed, grad, to_left, to_right,
    source, target, rel, tail, left_buf, right_buf, table_buf, own_buf, cotangent_buf, window,
    mixed_buf, grad_buf, grad_mixed_buf, state_buf, left_out, right_out, sems, *sums,
):
    long = window.shape[0] // 2
    far_sums(
        groups, long, 1, flat, tables, (left, right, near), (source, target, rel, tail),
        (left_buf, right_buf, table_buf), head_rows, window, sems, sums,
    )
    extra = fetch([(own, own_buf), (cotangent, cotangent_buf)], sems.at[pl.ds(8, 2)])
    walk(groups, tail[1], tail[3], source, target, rel, window, table_buf, sums)
    wait(extra)
    spread(own_buf, window, 0)
    spread(cotangent_buf, window, long)
    wide = split_weight(weights[1])
    wide_back = split_weight(weights[1].T)
    bias = biases[1]

    def step(i, carry):
        at = pl.multiple_of(i * DENSE, DENSE)
        rows = pl.ds(at, DENSE)
        mix = total_of(sums, at, DENSE)
        values = times(mix, wide) + bias
        sigma = jax.nn.sigmoid(values)
        window[rows, :] += values * sigma
        behind = pl.ds(long + at, DENSE)
        slope = window[behind, :] * (sigma * (1.0 + values * (1.0 - sigma)))
        back = times(slope, wide_back).astype(jnp.bfloat16)
        mixed_buf[rows, :] = mix
        grad_buf[rows, :] = slope
        grad_mixed_buf[rows, :] = back
        window[behind, :] = back.astype(jnp.float32)
        for ref in sums:
            ref[rows, :] = jnp.zeros((DENSE, LANES), jnp.float32)
            ref[behind, :] = jnp.zeros((DENSE, LANES), jnp.float32)
        return carry

    lax.fori_loop(0, long // DENSE, step, 0)
    size = CHUNK // groups

    def store(i, carry):
        at = pl.multiple_of(i * size, size)
        for j in range(groups):
            state_buf[pl.ds(at, size), j * LANES : (j + 1) * LANES] = window[
                pl.ds(at * groups + j, size, stride=groups), :
            ].astype(jnp.bfloat16)
        return carry

    lax.fori_loop(0, long // CHUNK, store, 0)
    stores = fetch(
        [(state_buf, state), (grad_mixed_buf, grad_mixed), (mixed_buf, mixed), (grad_buf, grad)],
        sems.at[pl.ds(10, 4)],
    )
    walk(
        groups, tail[1], tail[3], target, source, rel, window.at[pl.ds(long, long), :], table_buf, sums,
    )

    for k, (buf, out) in enumerate(((left_out, to_left), (right_out, to_right))):

        def total(i, carry):
            at = pl.multiple_of(i * CHUNK, CHUNK)
            buf[pl.ds(at, CHUNK), :] = total_of(sums, k * long + at).astype(jnp.bfloat16)
            return carry

        lax.fori_loop(0, long // CHUNK, total, 0)
        stores += fetch([(buf, out)], sems.at[pl.ds(14 + k, 1)])
    wait(stores)


def adjoint_kernel(
    groups, flat, grad_mixed, tables, cotangent, mixed, grad,
    base, to_mirror, weight_sum, bias_sum,
    source, target, rel, tail, grad_mixed_buf, table_buf, cotangent_buf, mixed_buf, grad_buf,
    mirror_out, window, wide_sum, sems, *sums,
):
    long = window.shape[0]
    lists = fetch_lists(flat, (source, target, rel, tail), tables, 1, table_buf, sems)
    loads = fetch([(grad_mixed, grad_mixed_buf)], sems.at[pl.ds(5, 1)])
    clear(sums)
    wait(loads)
    spread(grad_mixed_buf, window, 0)
    wait(lists)
    late = fetch(
        [(cotangent, cotangent_buf), (mixed, mixed_buf), (grad, grad_buf)], sems.at[pl.ds(6, 3)]
    )
    walk(groups, 0, tail[1], target, source, rel, window, table_buf, sums)

    def total(i, carry):
        at = pl.multiple_of(i * CHUNK, CHUNK)
        mirror_out[pl.ds(at, CHUNK), :] = total_of(sums, long + at).astype(jnp.bfloat16)
        return carry

    lax.fori_loop(0, long // CHUNK, total, 0)
    stores = fetch([(mirror_out, to_mirror)], sems.at[pl.ds(9, 1)])
    wait(late)
    spread(cotangent_buf, window, 0)
    wide_sum[...] = jnp.zeros_like(wide_sum)
    bias_sum[...] = jnp.zeros_like(bias_sum)

    def step(i, carry):
        at = pl.multiple_of(i * DENSE, DENSE)
        rows = pl.ds(at, DENSE)
        window[rows, :] += total_of(sums, at, DENSE)
        values = grad_buf[rows, :]
        wide_sum[...] += outer(mixed_buf[rows, :], values)
        bias_sum[...] += jnp.sum(values, axis=0, keepdims=True)
        return carry

    lax.fori_loop(0, long // DENSE, step, 0)
    stores += fetch([(window, base)], sems.at[pl.ds(10, 1)])
    weight_sum[...] = quarters(wide_sum[...])
    wait(stores)


def copy_kernel(source, out, sems):
    wait(fetch([(source, out)], sems))


def folded(wide):
    value = wide[:DIM, :DIM]
    for g in range(1, LANES // DIM):
        value = value + wide[g * DIM : (g + 1) * DIM, g * DIM : (g + 1) * DIM]
    return value


def folded_row(wide):
    value = wide[:, :DIM]
    for g in range(1, LANES // DIM):
        value = value + wide[:, g * DIM : (g + 1) * DIM]
    return value


def last_kernel(
    base, left, right, mirror, update, mixed, weight_one, bias_one, out, wide_sum, bias_sum
):
    @pl.when(pl.program_id(0) == 0)
    def _():
        wide_sum[...] = jnp.zeros_like(wide_sum)
        bias_sum[...] = jnp.zeros_like(bias_sum)

    state_grad = base[...]
    for ref in (left, right, mirror):
        state_grad = state_grad + ref[...].astype(jnp.float32)
    grad = state_grad * silu_slope(update[...])
    wide_sum[...] += outer(mixed[...], grad)
    bias_sum[...] += jnp.sum(grad, axis=0, keepdims=True)

    @pl.when(pl.program_id(0) == pl.num_programs(0) - 1)
    def _():
        out[...] = jnp.zeros_like(out)
        out[0:DIM, 0:DIM] = folded(quarters(wide_sum[...]))
        out[DIM : 2 * DIM, 0:DIM] = folded(weight_one[...])
        out[2 * DIM : 2 * DIM + 1, 0:DIM] = folded_row(bias_sum[...])
        out[2 * DIM + 1 : 2 * DIM + 2, 0:DIM] = folded_row(bias_one[...])


def edge_lists(edge_tiles, row_count, groups, rel_count):
    tile_count, _, slot_total = edge_tiles.shape
    lines = tile_count * slot_total // LANES
    row_bits = (row_count - 1).bit_length()
    room = (tile_count * slot_total + 5 * UNROLL + LINE - 1) // LINE * LINE
    flat = pltpu.VMEM((lines, LANES), jnp.int32)
    flat_smem = pltpu.SMEM((lines, LANES), jnp.int32)
    words, ends = pl.pallas_call(
        functools.partial(
            bucket_kernel, tile_count=tile_count, row_count=row_count, rel_count=rel_count
        ),
        out_shape=[jax.ShapeDtypeStruct((room,), jnp.int32), jax.ShapeDtypeStruct((4,), jnp.int32)],
        in_specs=[VMEM],
        out_specs=[SMEM] * 2,
        scratch_shapes=[flat] * 5
        + [pltpu.VMEM((8, LANES), jnp.int32), flat_smem, flat_smem]
        + [pltpu.SMEM((8, LANES), jnp.int32), pltpu.SemaphoreType.DMA((3,))],
        name="bucket",
    )(edge_tiles.transpose(1, 0, 2))
    source = (words & (2 * row_count - 1)) * groups
    target = ((words >> (row_bits + 1)) & (row_count - 1)) * groups
    return room, ends, source, target, words >> (2 * row_bits + 1)


def body(
    entity_state,
    edge_tiles,
    query_head,
    query_relation,
    query_table,
    rel_vectors,
    mix_weight,
    mix_bias,
    cotangent,
):
    row_count, col_count = entity_state.shape
    groups = col_count // LANES
    long = row_count * groups
    query_count = query_head.shape[0]
    rel_count = rel_vectors.shape[1]
    seats = Seats(lax.axis_size("node"), lax.axis_size("query"))

    def send(block, route):
        return lax.ppermute(block, AXES, route)

    def run(fn, args, specs, outs, out_specs, scratch):
        return pl.pallas_call(
            fn, out_shape=outs, in_specs=specs, out_specs=out_specs, scratch_shapes=scratch,
        )(*args)

    wide_f32 = jax.ShapeDtypeStruct((long, LANES), jnp.float32)
    wide_bf16 = jax.ShapeDtypeStruct((long, LANES), jnp.bfloat16)
    f32_buf = pltpu.VMEM((long, LANES), jnp.float32)
    bf16_buf = pltpu.VMEM((long, LANES), jnp.bfloat16)
    pair = pltpu.VMEM((2 * long, LANES), jnp.float32)
    sums = [f32_buf] * SUMS
    pair_sums = [pair] * SUMS
    square = jax.ShapeDtypeStruct((LANES, LANES), jnp.float32)
    line = jax.ShapeDtypeStruct((1, LANES), jnp.float32)

    state_zero = send(entity_state, seats.gather())
    room, ends, source, target, rel = edge_lists(edge_tiles, row_count, groups, rel_count)
    heads = query_head - lax.axis_index("node") * row_count
    tail = jnp.concatenate([ends, heads, query_relation])
    tail_room = -(-tail.shape[0] // LINE) * LINE
    tail = jnp.pad(tail, (0, tail_room - tail.shape[0]))
    flat = send(jnp.concatenate([source, target, rel, tail]), seats.gather())
    own_relation = flat[3 * room + 4 + query_count : 3 * room + 4 + 2 * query_count]
    grad_out = send(cotangent, seats.gather())

    choose_rel = (own_relation[:, None] == lax.iota(jnp.int32, query_table.shape[0])[None, :]).astype(
        jnp.float32
    )
    query_vec = (
        jnp.dot(choose_rel, query_table, precision=HIGHEST, preferred_element_type=jnp.float32)
        .astype(jnp.bfloat16)
        .astype(jnp.float32)
    )
    repeat = LANES // DIM
    lane_group = lax.iota(jnp.int32, LANES) // DIM
    head_rows = jnp.where(
        lane_group[None, :] == (lax.iota(jnp.int32, query_count) % repeat)[:, None],
        jnp.tile(query_vec, (1, repeat)),
        0.0,
    )
    tables = jnp.tile(jnp.pad(rel_vectors, ((0, 0), (0, -rel_count % 8 or 8), (0, 0))), (1, 1, repeat))
    same = lane_group[:, None] == lane_group[None, :]
    weights = jnp.where(same[None], jnp.tile(mix_weight, (1, repeat, repeat)), 0.0)
    biases = jnp.tile(mix_bias, (1, repeat))[:, None, :]
    list_bufs = [pltpu.SMEM((room,), jnp.int32)] * 3 + [pltpu.SMEM((tail_room,), jnp.int32)]
    table_buf = pltpu.VMEM(tables.shape[1:], jnp.float32)

    def sems(count):
        return pltpu.SemaphoreType.DMA((count,))

    def halo(state, index):
        buf = pltpu.VMEM(state.shape, jnp.bfloat16)
        mirror = send(state, seats.mirror())
        left = send(state, seats.shift(1))
        right = send(state, seats.shift(-1))
        near = run(
            functools.partial(near_kernel, groups, index),
            [flat, state, mirror, tables],
            [ANY] * 4,
            wide_f32,
            ANY,
            [*list_bufs, buf, buf, table_buf, pair, sems(11), *sums],
        )
        return left, right, near

    left, right, near = halo(state_zero, 0)
    block_buf = pltpu.VMEM(state_zero.shape, jnp.bfloat16)
    state_one, mixed_zero, update_zero = run(
        functools.partial(first_kernel, groups),
        [head_rows, weights, biases, flat, left, right, near, tables, state_zero],
        [VMEM] * 3 + [ANY] * 6,
        [wide_bf16, wide_f32, wide_f32],
        [ANY] * 3,
        [*list_bufs, block_buf, block_buf, table_buf, block_buf, pair, f32_buf, f32_buf, bf16_buf, sems(21)]
        + sums,
    )
    left, right, near = halo(state_one, 1)
    state_two, grad_mixed, mixed_one, grad_one, to_left, to_right = run(
        functools.partial(second_kernel, groups),
        [head_rows, weights, biases, flat, left, right, near, tables, state_one, grad_out],
        [VMEM] * 3 + [ANY] * 7,
        [jax.ShapeDtypeStruct(entity_state.shape, jnp.bfloat16), wide_bf16, wide_f32, wide_f32]
        + [wide_bf16] * 2,
        [ANY] * 6,
        [*list_bufs, bf16_buf, bf16_buf, table_buf, bf16_buf, block_buf, pair, f32_buf, f32_buf, bf16_buf]
        + [block_buf, bf16_buf, bf16_buf, sems(16), *pair_sums],
    )
    from_right = send(to_left, seats.shift(-1))
    from_left = send(to_right, seats.shift(1))
    final_state = run(
        copy_kernel, [send(state_two, seats.give_back())], [ANY],
        jax.ShapeDtypeStruct(entity_state.shape, jnp.bfloat16), VMEM, [sems(1)],
    )
    base, to_mirror, weight_one, bias_one = run(
        functools.partial(adjoint_kernel, groups),
        [flat, grad_mixed, tables, grad_out, mixed_one, grad_one],
        [ANY] * 6,
        [wide_f32, wide_bf16, square, line],
        [ANY] * 2 + [VMEM] * 2,
        [*list_bufs, bf16_buf, table_buf, block_buf, f32_buf, f32_buf, bf16_buf, f32_buf]
        + [pltpu.VMEM((2 * LANES, 2 * LANES), jnp.float32), sems(11), *pair_sums],
    )
    from_mirror = send(to_mirror, seats.mirror())
    steps = 4
    rows = pl.BlockSpec((long // steps, LANES), lambda i: (i, 0))
    whole = lambda shape: pl.BlockSpec(shape, lambda i: (0, 0))
    grads = pl.pallas_call(
        last_kernel,
        out_shape=jax.ShapeDtypeStruct((2 * DIM + 8, LANES), jnp.float32),
        grid=(steps,),
        in_specs=[rows] * 6 + [whole((LANES, LANES)), whole((1, LANES))],
        out_specs=whole((2 * DIM + 8, LANES)),
        scratch_shapes=[
            pltpu.VMEM((2 * LANES, 2 * LANES), jnp.float32),
            pltpu.VMEM((1, LANES), jnp.float32),
        ],
        name="last",
    )(base, from_left, from_right, from_mirror, update_zero, mixed_zero, weight_one, bias_one)
    devices = seats.nodes * seats.queries
    reach = 1
    while reach < devices:
        grads = grads + send(grads, [(i, i ^ reach) for i in range(devices)])
        reach *= 2
    weight_grads = grads[: 2 * DIM, :DIM].reshape(2, DIM, DIM)
    bias_grads = grads[2 * DIM : 2 * DIM + 2, :DIM]
    return (final_state, weight_grads, bias_grads)


def solution(mesh):
    placed = (
        P("node", "query"),
        P("node", None, None),
        P("query"),
        P("query"),
        P(),
        P(),
        P(),
        P(),
        P("node", "query"),
    )

    return jax.shard_map(
        body, mesh=mesh, in_specs=placed, out_specs=(P("node", "query"), P(), P()), check_vma=False
    )
```

profile of v0, /device:TPU:10, one launch (start us, length us, event | category | flops | bytes accessed | tf_op | source)
XLA Modules:
  0.0 204.6 jit_solution(5982267883729270350)
XLA Ops:
  0.7 2.6 %collective-permute-start.1 = (bf16[1024,512]{1,0:T(8,128)(2,1)}, bf16[1024,512]{1,0:T(8,128)(2,1)S(1)}, u32[]{:S(2)}, u32[]{:S(2)}) collective-permute-start(bf16[1024,512]{1,0:T(8,128)(2,1)} %param.9), channel_id=1, source_target_pairs={{0,0},{1,16},{2,2},{3,18},{4,4},{5,20},{6,6},{7,22},{8,12},{9,28},... | collective-permute-start | bytes 3145736 | tf_op jit(solution)/shard_map/ppermute | solution.py:546
  3.9 17.9 %bucket.1 = (s32[9216]{0:T(1024)}, s32[4]{0:T(128)}) custom-call(s32[3,16,512]{2,1,0:T(8,128)} %bitcast.5), custom_call_target="tpu_custom_call" | custom-call | tf_op jit(solution)/shard_map/bucket/pallas_call | solution.py:510
  24.0 3.4 %collective-permute-start = (s32[28672]{0:T(1024)}, s32[28672]{0:T(1024)S(1)}, u32[]{:S(2)}, u32[]{:S(2)}) collective-permute-start(s32[28672]{0:T(1024)} %pad_add_fusion), channel_id=1, source_target_pairs={{0,0},{1,16},{2,2},{3,18},{4,4},{5,20},{6,6},{7,22},{8,12},{9,28},... | collective-permute-start | bytes 344072 | tf_op jit(solution)/shard_map/ppermute | solution.py:546
  27.4 1.5 collective-permute-done.1.own
  29.8 1.4 collective-permute-start.2
  37.7 12.0 %shard_map.112.near = f32[4096,128]{1,0:T(8,128)} custom-call(s32[28672]{0:T(1024)} %copy-done.3, bf16[1024,512]{1,0:T(8,128)(2,1)} %copy-done.1, bf16[1024,512]{1,0:T(8,128)(2,1)} %copy-done.4, f32[2,824,128]{2,1,0:T(8,128)} %copy.13.tables), custom_call_target="tpu_custom_call" | custom-call | tf_op jit(solution)/shard_map/pallas_call | solution.py:549
  49.7 6.2 %collective-permute-done.3.right = bf16[1024,512]{1,0:T(8,128)(2,1)} collective-permute-done((bf16[1024,512]{1,0:T(8,128)(2,1)S(1)}, bf16[1024,512]{1,0:T(8,128)(2,1)}, u32[]{:S(2)}, u32[]{:S(2)}) %collective-permute-start.3) | collective-permute-done | bytes 1048608 | tf_op jit(solution)/shard_map/ppermute | solution.py:546
  55.8 14.8 %shard_map.113 = (bf16[4096,128]{1,0:T(8,128)(2,1)}, f32[4096,128]{1,0:T(8,128)}, f32[4096,128]{1,0:T(8,128)}) custom-call(f32[16,128]{1,0:T(8,128)} %compare_select_fusion.head_rows, f32[2,128,128]{2,1,0:T(8,128)} %broadcast_select_fusion.weights, f32[2,1,128]{2,1,0:T(1,128)} %tile.40.biases, s32[28672]{0:T(1024)} %copy-done.3, ...), custom_call_target="tpu_custom_call" | custom-call | tf_op jit(solution)/shard_map/pallas_call | solution.py:549
  70.7 3.7 %collective-permute-start.8 = (bf16[1024,512]{1,0:T(8,128)(2,1)}, bf16[1024,512]{1,0:T(8,128)(2,1)S(1)}, u32[]{:S(2)}, u32[]{:S(2)}) collective-permute-start(bf16[1024,512]{1,0:T(8,128)(2,1)} %param.17), channel_id=1, source_target_pairs={{0,0},{1,16},{2,2},{3,18},{4,4},{5,20},{6,6},{7,22},{8,12},{9,28},... | collective-permute-start | bytes 3145736 | tf_op jit(solution)/shard_map/ppermute | solution.py:546
  74.5 2.0 collective-permute-start.5
  77.5 12.0 %shard_map.114.near = f32[4096,128]{1,0:T(8,128)} custom-call(s32[28672]{0:T(1024)} %copy-done.3, bf16[4096,128]{1,0:T(8,128)(2,1)} %get-tuple-element.20.own, bf16[4096,128]{1,0:T(8,128)(2,1)} %copy-done.8, f32[2,824,128]{2,1,0:T(8,128)} %copy.13.tables), custom_call_target="tpu_custom_call" | custom-call | tf_op jit(solution)/shard_map/pallas_call | solution.py:549
  89.5 18.6 %collective-permute-done.8.cotangent = bf16[1024,512]{1,0:T(8,128)(2,1)S(1)} collective-permute-done((bf16[1024,512]{1,0:T(8,128)(2,1)}, bf16[1024,512]{1,0:T(8,128)(2,1)S(1)}, u32[]{:S(2)}, u32[]{:S(2)}) %collective-permute-start.8) | collective-permute-done | bytes 1048608 | tf_op jit(solution)/shard_map/ppermute | solution.py:546
  108.1 13.2 %collective-permute-done.6.right = bf16[4096,128]{1,0:T(8,128)(2,1)S(1)} collective-permute-done((bf16[4096,128]{1,0:T(8,128)(2,1)}, bf16[4096,128]{1,0:T(8,128)(2,1)S(1)}, u32[]{:S(2)}, u32[]{:S(2)}) %collective-permute-start.6) | collective-permute-done | bytes 1048608 | tf_op jit(solution)/shard_map/ppermute | solution.py:546
  122.3 25.6 %shard_map.115 = (bf16[1024,512]{1,0:T(8,128)(2,1)}, bf16[4096,128]{1,0:T(8,128)(2,1)}, f32[4096,128]{1,0:T(8,128)}, f32[4096,128]{1,0:T(8,128)}, bf16[4096,128]{1,0:T(8,128)(2,1)}, /*index=5*/bf16[4096,128]{1,0:T(8,128)(2,1)}) custom-call(f32[16,128]{1,0:T(8,128)} %compare_select_fusion.head_rows, f32[2,128,128]{2,1,0:T(8,128)} %broadcast_select_fusion.weights, ...), custom_call_target="tpu_custom_call" | custom-call | tf_op jit(solution)/shard_map/pallas_call | solution.py:549
  149.9 15.6 %shard_map.117 = (f32[4096,128]{1,0:T(8,128)}, bf16[4096,128]{1,0:T(8,128)(2,1)}, f32[128,128]{1,0:T(8,128)}, f32[1,128]{1,0:T(1,128)}) custom-call(s32[28672]{0:T(1024)} %copy-done.3, bf16[4096,128]{1,0:T(8,128)(2,1)} %get-tuple-element.22.grad_mixed, f32[2,824,128]{2,1,0:T(8,128)} %copy.13.tables, bf16[1024,512]{1,0:T(8,128)(2,1)} %copy-done.2, ...), custom_call_target="tpu_custom_call" | custom-call | tf_op jit(solution)/shard_map/pallas_call | solution.py:549
  165.6 3.0 %collective-permute-start.9 = (bf16[1024,512]{1,0:T(8,128)(2,1)}, bf16[1024,512]{1,0:T(8,128)(2,1)}, u32[]{:S(2)}, u32[]{:S(2)}) collective-permute-start(bf16[1024,512]{1,0:T(8,128)(2,1)} %get-tuple-element.21), channel_id=1, source_target_pairs={{0,0},{16,1},{2,2},{18,3},{4,4},{20,5},{6,6},{22,7},{12,8},{28,9},... | collective-permute-start | bytes 3145736 | tf_op jit(solution)/shard_map/ppermute | solution.py:546
  170.3 6.0 %last.1 = f32[72,128]{1,0:T(8,128)} custom-call(f32[4096,128]{1,0:T(8,128)} %get-tuple-element.25.base, bf16[4096,128]{1,0:T(8,128)(2,1)} %copy-done.5, bf16[4096,128]{1,0:T(8,128)(2,1)} %copy-done.6, bf16[4096,128]{1,0:T(8,128)(2,1)} %copy-done.7, f32[4096,128]{1,0:T(8,128)} %get-tuple-element.29.update, f32[4096,128]{1,0:T(8,128)} %get-tuple-element.30.mixed, ...), custom_call_target="tpu_custom_call" | custom-call | tf_op jit(solution)/shard_map/last/pallas_call | solution.py:654
  178.5 1.5 collective-permute-start.14
  180.1 2.4 %collective-permute-done.14 = f32[72,128]{1,0:T(8,128)S(1)} collective-permute-done((f32[72,128]{1,0:T(8,128)S(1)}, f32[72,128]{1,0:T(8,128)S(1)}, u32[]{:S(2)}, u32[]{:S(2)}) %collective-permute-start.14) | collective-permute-done | bytes 36896 | tf_op jit(solution)/shard_map/ppermute | solution.py:546
  183.5 11.1 %collective-permute-done.15 = f32[72,128]{1,0:T(8,128)S(1)} collective-permute-done((f32[72,128]{1,0:T(8,128)S(1)}, f32[72,128]{1,0:T(8,128)S(1)}, u32[]{:S(2)}, u32[]{:S(2)}) %collective-permute-start.15) | collective-permute-done | bytes 36896 | tf_op jit(solution)/shard_map/ppermute | solution.py:546
  194.6 3.9 %collective-permute-done.16 = f32[72,128]{1,0:T(8,128)S(1)} collective-permute-done((f32[72,128]{1,0:T(8,128)S(1)}, f32[72,128]{1,0:T(8,128)S(1)}, u32[]{:S(2)}, u32[]{:S(2)}) %collective-permute-start.16) | collective-permute-done | bytes 36896 | tf_op jit(solution)/shard_map/ppermute | solution.py:546
  198.5 1.3 collective-permute-start.17
  199.8 2.2 %shard_map.116 = bf16[1024,512]{1,0:T(8,128)(2,1)} custom-call(bf16[1024,512]{1,0:T(8,128)(2,1)} %collective-permute-done.9.source), custom_call_target="tpu_custom_call" | custom-call | tf_op jit(solution)/shard_map/pallas_call | solution.py:549
  202.0 1.4 collective-permute-done.17
  (69 shorter events, 20.4 us)
Async XLA Ops:
  0.6 35.1 %copy-start = (f32[822,32]{0,1:T(8,128)S(1)}, f32[822,32]{0,1:T(8,128)}, u32[]{:S(2)}) copy-start(f32[822,32]{0,1:T(8,128)} %param.13) | copy-start | bytes 315652
  0.6 33.7 %copy-start.10 = (f32[2,822,32]{1,2,0:T(8,128)S(1)}, f32[2,822,32]{1,2,0:T(8,128)}, u32[]{:S(2)}) copy-start(f32[2,822,32]{1,2,0:T(8,128)} %param.14) | copy-start | bytes 631300
  0.7 28.3 %collective-permute-start.1 = (bf16[1024,512]{1,0:T(8,128)(2,1)}, bf16[1024,512]{1,0:T(8,128)(2,1)S(1)}, u32[]{:S(2)}, u32[]{:S(2)}) collective-permute-start(bf16[1024,512]{1,0:T(8,128)(2,1)} %param.9), channel_id=1, source_target_pairs={{0,0},{1,16},{2,2},{3,18},{4,4},{5,20},{6,6},{7,22},{8,12},{9,28},... | collective-permute-start | bytes 3145736 | tf_op jit(solution)/shard_map/ppermute | solution.py:546
  24.0 11.6 %collective-permute-start = (s32[28672]{0:T(1024)}, s32[28672]{0:T(1024)S(1)}, u32[]{:S(2)}, u32[]{:S(2)}) collective-permute-start(s32[28672]{0:T(1024)} %pad_add_fusion), channel_id=1, source_target_pairs={{0,0},{1,16},{2,2},{3,18},{4,4},{5,20},{6,6},{7,22},{8,12},{9,28},... | collective-permute-start | bytes 344072 | tf_op jit(solution)/shard_map/ppermute | solution.py:546
  28.9 6.7 %copy-start.1 = (bf16[1024,512]{1,0:T(8,128)(2,1)}, bf16[1024,512]{1,0:T(8,128)(2,1)S(1)}, u32[]{:S(2)}) copy-start(bf16[1024,512]{1,0:T(8,128)(2,1)S(1)} %collective-permute-done.1.own) | copy-start | bytes 3145732
  28.9 7.8 %collective-permute-start.4 = (bf16[1024,512]{1,0:T(8,128)(2,1)S(1)}, bf16[1024,512]{1,0:T(8,128)(2,1)S(1)}, u32[]{:S(2)}, u32[]{:S(2)}) collective-permute-start(bf16[1024,512]{1,0:T(8,128)(2,1)S(1)} %collective-permute-done.1.own), channel_id=1, source_target_pairs={{0,1},{16,17},{2,3},{18,19},{4,5},{20,21},{6,7},{22,23},{12,13},{2... | collective-permute-start | bytes 3145736 | tf_op jit(solution)/shard_map/ppermute | solution.py:546
  29.1 26.7 %collective-permute-start.3 = (bf16[1024,512]{1,0:T(8,128)(2,1)S(1)}, bf16[1024,512]{1,0:T(8,128)(2,1)}, u32[]{:S(2)}, u32[]{:S(2)}) collective-permute-start(bf16[1024,512]{1,0:T(8,128)(2,1)S(1)} %collective-permute-done.1.own), channel_id=1, source_target_pairs={{4,0},{20,16},{6,2},{22,18},{12,4},{28,20},{14,6},{30,22},{8,12},{... | collective-permute-start | bytes 3145736 | tf_op jit(solution)/shard_map/ppermute | solution.py:546
  29.8 26.1 %collective-permute-start.2 = (bf16[1024,512]{1,0:T(8,128)(2,1)S(1)}, bf16[1024,512]{1,0:T(8,128)(2,1)}, u32[]{:S(2)}, u32[]{:S(2)}) collective-permute-start(bf16[1024,512]{1,0:T(8,128)(2,1)S(1)} %collective-permute-done.1.own), channel_id=1, source_target_pairs={{9,0},{25,16},{11,2},{27,18},{0,4},{16,20},{2,6},{18,22},{4,12},{2... | collective-permute-start | bytes 3145736 | tf_op jit(solution)/shard_map/ppermute | solution.py:546
  70.6 5.9 %collective-permute-start.7 = (bf16[4096,128]{1,0:T(8,128)(2,1)}, bf16[4096,128]{1,0:T(8,128)(2,1)S(1)}, u32[]{:S(2)}, u32[]{:S(2)}) collective-permute-start(bf16[4096,128]{1,0:T(8,128)(2,1)} %get-tuple-element.20.own), channel_id=1, source_target_pairs={{0,1},{16,17},{2,3},{18,19},{4,5},{20,21},{6,7},{22,23},{12,13},{2... | collective-permute-start | bytes 3145736 | tf_op jit(solution)/shard_map/ppermute | solution.py:546
  70.7 37.4 %collective-permute-start.8 = (bf16[1024,512]{1,0:T(8,128)(2,1)}, bf16[1024,512]{1,0:T(8,128)(2,1)S(1)}, u32[]{:S(2)}, u32[]{:S(2)}) collective-permute-start(bf16[1024,512]{1,0:T(8,128)(2,1)} %param.17), channel_id=1, source_target_pairs={{0,0},{1,16},{2,2},{3,18},{4,4},{5,20},{6,6},{7,22},{8,12},{9,28},... | collective-permute-start | bytes 3145736 | tf_op jit(solution)/shard_map/ppermute | solution.py:546
  74.4 46.9 %collective-permute-start.6 = (bf16[4096,128]{1,0:T(8,128)(2,1)}, bf16[4096,128]{1,0:T(8,128)(2,1)S(1)}, u32[]{:S(2)}, u32[]{:S(2)}) collective-permute-start(bf16[4096,128]{1,0:T(8,128)(2,1)} %get-tuple-element.20.own), channel_id=1, source_target_pairs={{4,0},{20,16},{6,2},{22,18},{12,4},{28,20},{14,6},{30,22},{8,12},{... | collective-permute-start | bytes 3145736 | tf_op jit(solution)/shard_map/ppermute | solution.py:546
  74.5 46.8 %collective-permute-start.5 = (bf16[4096,128]{1,0:T(8,128)(2,1)}, bf16[4096,128]{1,0:T(8,128)(2,1)}, u32[]{:S(2)}, u32[]{:S(2)}) collective-permute-start(bf16[4096,128]{1,0:T(8,128)(2,1)} %get-tuple-element.20.own), channel_id=1, source_target_pairs={{9,0},{25,16},{11,2},{27,18},{0,4},{16,20},{2,6},{18,22},{4,12},{2... | collective-permute-start | bytes 3145736 | tf_op jit(solution)/shard_map/ppermute | solution.py:546
  108.1 13.2 %copy-start.2 = (bf16[1024,512]{1,0:T(8,128)(2,1)}, bf16[1024,512]{1,0:T(8,128)(2,1)S(1)}, u32[]{:S(2)}) copy-start(bf16[1024,512]{1,0:T(8,128)(2,1)S(1)} %collective-permute-done.8.cotangent) | copy-start | bytes 3145732
  147.8 20.8 %collective-permute-start.10 = (bf16[4096,128]{1,0:T(8,128)(2,1)}, bf16[4096,128]{1,0:T(8,128)(2,1)S(1)}, u32[]{:S(2)}, u32[]{:S(2)}) collective-permute-start(bf16[4096,128]{1,0:T(8,128)(2,1)} %get-tuple-element.26), channel_id=1, source_target_pairs={{9,0},{25,16},{11,2},{27,18},{0,4},{16,20},{2,6},{18,22},{4,12},{2... | collective-permute-start | bytes 3145736 | tf_op jit(solution)/shard_map/ppermute | solution.py:546
  149.0 19.6 %collective-permute-start.11 = (bf16[4096,128]{1,0:T(8,128)(2,1)}, bf16[4096,128]{1,0:T(8,128)(2,1)S(1)}, u32[]{:S(2)}, u32[]{:S(2)}) collective-permute-start(bf16[4096,128]{1,0:T(8,128)(2,1)} %get-tuple-element.27), channel_id=1, source_target_pairs={{4,0},{20,16},{6,2},{22,18},{12,4},{28,20},{14,6},{30,22},{8,12},{... | collective-permute-start | bytes 3145736 | tf_op jit(solution)/shard_map/ppermute | solution.py:546
  165.5 3.1 %collective-permute-start.12 = (bf16[4096,128]{1,0:T(8,128)(2,1)}, bf16[4096,128]{1,0:T(8,128)(2,1)S(1)}, u32[]{:S(2)}, u32[]{:S(2)}) collective-permute-start(bf16[4096,128]{1,0:T(8,128)(2,1)} %get-tuple-element.28), channel_id=1, source_target_pairs={{0,1},{16,17},{2,3},{18,19},{4,5},{20,21},{6,7},{22,23},{12,13},{2... | collective-permute-start | bytes 3145736 | tf_op jit(solution)/shard_map/ppermute | solution.py:546
  165.6 34.2 %collective-permute-start.9 = (bf16[1024,512]{1,0:T(8,128)(2,1)}, bf16[1024,512]{1,0:T(8,128)(2,1)}, u32[]{:S(2)}, u32[]{:S(2)}) collective-permute-start(bf16[1024,512]{1,0:T(8,128)(2,1)} %get-tuple-element.21), channel_id=1, source_target_pairs={{0,0},{16,1},{2,2},{18,3},{4,4},{20,5},{6,6},{22,7},{12,8},{28,9},... | collective-permute-start | bytes 3145736 | tf_op jit(solution)/shard_map/ppermute | solution.py:546
  168.7 1.4 copy-start.6
  168.7 1.6 copy-start.7
  176.3 1.4 collective-permute-start.13
  178.5 4.0 %collective-permute-start.14 = (f32[72,128]{1,0:T(8,128)S(1)}, f32[72,128]{1,0:T(8,128)S(1)}, u32[]{:S(2)}, u32[]{:S(2)}) collective-permute-start(f32[72,128]{1,0:T(8,128)S(1)} %add.39), channel_id=1, source_target_pairs={{0,2},{1,3},{2,0},{3,1},{4,6},{5,7},{6,4},{7,5},{8,10},{9,11},{10,... | collective-permute-start | bytes 110600 | tf_op jit(solution)/shard_map/ppermute | solution.py:546
  182.5 12.1 %collective-permute-start.15 = (f32[72,128]{1,0:T(8,128)S(1)}, f32[72,128]{1,0:T(8,128)S(1)}, u32[]{:S(2)}, u32[]{:S(2)}) collective-permute-start(f32[72,128]{1,0:T(8,128)S(1)} %add.40), channel_id=1, source_target_pairs={{0,4},{1,5},{2,6},{3,7},{4,0},{5,1},{6,2},{7,3},{8,12},{9,13},{10,... | collective-permute-start | bytes 110600 | tf_op jit(solution)/shard_map/ppermute | solution.py:546
  194.6 4.0 %collective-permute-start.16 = (f32[72,128]{1,0:T(8,128)S(1)}, f32[72,128]{1,0:T(8,128)S(1)}, u32[]{:S(2)}, u32[]{:S(2)}) collective-permute-start(f32[72,128]{1,0:T(8,128)S(1)} %add.41), channel_id=1, source_target_pairs={{0,8},{1,9},{2,10},{3,11},{4,12},{5,13},{6,14},{7,15},{8,0},{9,1},... | collective-permute-start | bytes 110600 | tf_op jit(solution)/shard_map/ppermute | solution.py:546
  198.5 4.9 %collective-permute-start.17 = (f32[72,128]{1,0:T(8,128)S(1)}, f32[72,128]{1,0:T(8,128)S(1)}, u32[]{:S(2)}, u32[]{:S(2)}) collective-permute-start(f32[72,128]{1,0:T(8,128)S(1)} %add.42), channel_id=1, source_target_pairs={{0,16},{1,17},{2,18},{3,19},{4,20},{5,21},{6,22},{7,23},{8,24},{9,... | collective-permute-start | bytes 110600 | tf_op jit(solution)/shard_map/ppermute | solution.py:546
  (5 other events, 5.0 us)
where the time goes:
time: 208 us; the launch traced here: 205 us
  Pallas kernels  106 us (51%)
  waiting for transfers between devices  59.6 us (29%)
  starting transfers between devices  23.2 us (11%)
  local copies, waits for them, and re-layouts  9.59 us (5%)
  other arithmetic  5.07 us (2%)
    pallas_call x6, Pallas kernels, run(): pl.pallas_call(fn, out_shape=outs, in_specs=specs, out_specs=out_specs, s...  82.1 us
    ppermute x18, waiting for transfers between devices, send(): return lax.ppermute(block, AXES, route)  59.6 us
    ppermute x18, starting transfers between devices, send(): return lax.ppermute(block, AXES, route)  23.2 us
    pallas_call x1, Pallas kernels, edge_lists(): pl.pallas_call(functools.partial(bucket_kernel, tile_count=tile_count, ro...  17.9 us
    pallas_call x1, Pallas kernels, body(): pl.pallas_call(last_kernel, out_shape=jax.ShapeDtypeStruct((2 * DIM + 8,...  6.05 us
    unnamed x22, local copies, waits for them, and re-layouts  4.54 us
  transfers between devices with their start and end apart: 18, of which 9 were waited for; matrix products, arithmetic and copies ran while one was open for 4% of the time, Pallas kernels for 32%

commit v1 on v0

--- a/solution.py
+++ b/solution.py
@@ -231,12 +231,46 @@
     )
 
 
-def near_kernel(
-    groups, index, flat, own, mirror, tables, out,
+def update_of(mixed, wide, bias):
+    both = jnp.dot(mixed, wide, preferred_element_type=jnp.float32)
+    return both[:, :LANES] + both[:, LANES:] + bias
+
+
+def advance(state_buf, mixed_buf, window, first, wide, bias):
+    spread(state_buf, window, first)
+
+    def step(i, carry):
+        at = pl.multiple_of(i * DENSE, DENSE)
+        values = update_of(mixed_buf[pl.ds(at, DENSE), :], wide, bias)
+        window[pl.ds(first + at, DENSE), :] += values * jax.nn.sigmoid(values)
+        return carry
+
+    lax.fori_loop(0, mixed_buf.shape[0] // DENSE, step, 0)
+
+
+def send_total(sums, out, sems):
+    parts = 4
+    size = sums[0].shape[0] // parts
+    stores = []
+    for k in range(parts):
+
+        def step(i, carry):
+            at = pl.multiple_of(k * size + i * CHUNK, CHUNK)
+            sums[0][pl.ds(at, CHUNK), :] = total_of(sums, at)
+            return carry
+
+        lax.fori_loop(0, size // CHUNK, step, 0)
+        piece = pl.ds(k * size, size)
+        stores += fetch([(sums[0].at[piece, :], out.at[piece, :])], sems.at[pl.ds(k, 1)])
+    wait(stores)
+
+
+def near_zero_kernel(
+    groups, flat, own, mirror, tables, out,
     source, target, rel, tail, own_buf, mirror_buf, table_buf, window, sems, *sums,
 ):
     long = sums[0].shape[0]
-    lists = fetch_lists(flat, (source, target, rel, tail), tables, index, table_buf, sems)
+    lists = fetch_lists(flat, (source, target, rel, tail), tables, 0, table_buf, sems)
     states = fetch([(own, own_buf), (mirror, mirror_buf)], sems.at[pl.ds(5, 2)])
     clear(sums)
     states[0].wait()
@@ -245,20 +279,25 @@
     spread(mirror_buf, window, long)
     wait(lists)
     walk(groups, 0, tail[1], source, target, rel, window, table_buf, sums)
-    parts = 4
-    size = long // parts
-    stores = []
-    for k in range(parts):
-
-        def step(i, carry):
-            at = pl.multiple_of(k * size + i * CHUNK, CHUNK)
-            sums[0][pl.ds(at, CHUNK), :] = total_of(sums, at)
-            return carry
-
-        lax.fori_loop(0, size // CHUNK, step, 0)
-        piece = pl.ds(k * size, size)
-        stores += fetch([(sums[0].at[piece, :], out.at[piece, :])], sems.at[pl.ds(7 + k, 1)])
-    wait(stores)
+    send_total(sums, out, sems.at[pl.ds(7, 4)])
+
+
+def near_one_kernel(
+    groups, weights, biases, flat, own, mirror, mirror_mixed, tables, out,
+    source, target, rel, tail, own_buf, mirror_buf, mixed_buf, table_buf, window, sems, *sums,
+):
+    long = sums[0].shape[0]
+    lists = fetch_lists(flat, (source, target, rel, tail), tables, 1, table_buf, sems)
+    states = fetch(
+        [(own, own_buf), (mirror, mirror_buf), (mirror_mixed, mixed_buf)], sems.at[pl.ds(5, 3)]
+    )
+    clear(sums)
+    wait(states)
+    spread(own_buf, window, 0)
+    advance(mirror_buf, mixed_buf, window, long, split(weights[0]), biases[0])
+    wait(lists)
+    walk(groups, 0, tail[1], source, target, rel, window, table_buf, sums)
+    send_total(sums, out, sems.at[pl.ds(8, 4)])
 
 
 def add_boundary(groups, heads, head_rows, ref, long):
@@ -277,36 +316,23 @@
     return fetch(pairs + [(tables.at[index], table_buf)], sems)
 
 
-def far_sums(groups, long, index, flat, tables, states, list_bufs, bufs, head_rows, window, sems, sums):
-    left, right, near = states
-    left_buf, right_buf, table_buf = bufs
-    lists = fetch_lists(flat, list_bufs, tables, index, table_buf, sems)
-    states = fetch(
-        [(left, left_buf), (right, right_buf), (near, sums[0].at[pl.ds(0, long), :])],
-        sems.at[pl.ds(5, 3)],
-    )
-    clear([ref.at[pl.ds(0, long), :] for ref in sums[1:]])
+def first_kernel(
+    groups, head_rows, weights, biases, flat, left, right, near, tables, own, state, mixed,
+    source, target, rel, tail, left_buf, right_buf, table_buf, own_buf, window, mixed_buf, state_buf,
+    sems, *sums,
+):
+    long = sums[0].shape[0]
+    lists = fetch_lists(flat, (source, target, rel, tail), tables, 0, table_buf, sems)
+    states = fetch([(left, left_buf), (right, right_buf), (near, sums[0])], sems.at[pl.ds(5, 3)])
+    clear(sums[1:])
     states[0].wait()
     spread(left_buf, window, 0)
     states[1].wait()
     spread(right_buf, window, long)
     states[2].wait()
     wait(lists)
-    _, _, _, tail = list_bufs
+    extra = fetch([(own, own_buf)], sems.at[pl.ds(8, 1)])
     add_boundary(groups, tail, head_rows, sums[0], long)
-
-
-def first_kernel(
-    groups, head_rows, weights, biases, flat, left, right, near, tables, own, state, mixed, update,
-    source, target, rel, tail, left_buf, right_buf, table_buf, own_buf, window, mixed_buf, update_buf,
-    state_buf, sems, *sums,
-):
-    long = sums[0].shape[0]
-    far_sums(
-        groups, long, 0, flat, tables, (left, right, near), (source, target, rel, tail),
-        (left_buf, right_buf, table_buf), head_rows, window, sems, sums,
-    )
-    extra = fetch([(own, own_buf)], sems.at[pl.ds(8, 1)])
     walk(groups, tail[1], tail[3], source, target, rel, window, table_buf, sums)
     wait(extra)
     spread(own_buf, window, 0)
@@ -322,8 +348,7 @@
             rows = pl.ds(at, DENSE)
             mix = total_of(sums, at, DENSE)
             values = times(mix, wide) + bias
-            mixed_buf[rows, :] = mix
-            update_buf[rows, :] = values
+            mixed_buf[rows, :] = mix.astype(jnp.bfloat16)
             state_buf[rows, :] = (window[rows, :] + values * jax.nn.sigmoid(values)).astype(
                 jnp.bfloat16
             )
@@ -332,28 +357,34 @@
         lax.fori_loop(0, size // DENSE, step, 0)
         rows = pl.ds(k * size, size)
         stores += fetch(
-            [
-                (state_buf.at[rows, :], state.at[rows, :]),
-                (mixed_buf.at[rows, :], mixed.at[rows, :]),
-                (update_buf.at[rows, :], update.at[rows, :]),
-            ],
-            sems.at[pl.ds(9 + 3 * k, 3)],
+            [(state_buf.at[rows, :], state.at[rows, :]), (mixed_buf.at[rows, :], mixed.at[rows, :])],
+            sems.at[pl.ds(9 + 2 * k, 2)],
         )
     wait(stores)
 
 
 def second_kernel(
-    groups, head_rows, weights, biases, flat, left, right, near, tables, own, cotangent,
-    state, grad_mixed, mixed, grad, to_left, to_right,
-    source, target, rel, tail, left_buf, right_buf, table_buf, own_buf, cotangent_buf, window,
-    mixed_buf, grad_buf, grad_mixed_buf, state_buf, left_out, right_out, sems, *sums,
+    groups, head_rows, weights, biases, flat, left, right, left_mixed, right_mixed, near, tables, own,
+    cotangent, state, grad_mixed, weight_sum, bias_sum,
+    source, target, rel, tail, left_buf, right_buf, left_mixed_buf, right_mixed_buf, table_buf, own_buf,
+    cotangent_buf, window, grad_mixed_buf, state_buf, wide_sum, sems, *sums,
 ):
-    long = window.shape[0] // 2
-    far_sums(
-        groups, long, 1, flat, tables, (left, right, near), (source, target, rel, tail),
-        (left_buf, right_buf, table_buf), head_rows, window, sems, sums,
-    )
-    extra = fetch([(own, own_buf), (cotangent, cotangent_buf)], sems.at[pl.ds(8, 2)])
+    long = sums[0].shape[0]
+    states = fetch(
+        [(left, left_buf), (left_mixed, left_mixed_buf), (right, right_buf)]
+        + [(right_mixed, right_mixed_buf), (near, sums[0])],
+        sems.at[pl.ds(5, 5)],
+    )
+    lists = fetch_lists(flat, (source, target, rel, tail), tables, 1, table_buf, sems)
+    clear(sums[1:])
+    first = split(weights[0])
+    wait(states[:2])
+    advance(left_buf, left_mixed_buf, window, 0, first, biases[0])
+    wait(states[2:])
+    advance(right_buf, right_mixed_buf, window, long, first, biases[0])
+    wait(lists)
+    extra = fetch([(own, own_buf), (cotangent, cotangent_buf)], sems.at[pl.ds(10, 2)])
+    add_boundary(groups, tail, head_rows, sums[0], long)
     walk(groups, tail[1], tail[3], source, target, rel, window, table_buf, sums)
     wait(extra)
     spread(own_buf, window, 0)
@@ -361,6 +392,8 @@
     wide = split_weight(weights[1])
     wide_back = split_weight(weights[1].T)
     bias = biases[1]
+    wide_sum[...] = jnp.zeros_like(wide_sum)
+    bias_sum[...] = jnp.zeros_like(bias_sum)
 
     def step(i, carry):
         at = pl.multiple_of(i * DENSE, DENSE)
@@ -369,19 +402,14 @@
         values = times(mix, wide) + bias
         sigma = jax.nn.sigmoid(values)
         window[rows, :] += values * sigma
-        behind = pl.ds(long + at, DENSE)
-        slope = window[behind, :] * (sigma * (1.0 + values * (1.0 - sigma)))
-        back = times(slope, wide_back).astype(jnp.bfloat16)
-        mixed_buf[rows, :] = mix
-        grad_buf[rows, :] = slope
-        grad_mixed_buf[rows, :] = back
-        window[behind, :] = back.astype(jnp.float32)
-        for ref in sums:
-            ref[rows, :] = jnp.zeros((DENSE, LANES), jnp.float32)
-            ref[behind, :] = jnp.zeros((DENSE, LANES), jnp.float32)
+        grad = window[pl.ds(long + at, DENSE), :] * (sigma * (1.0 + values * (1.0 - sigma)))
+        grad_mixed_buf[rows, :] = times(grad, wide_back).astype(jnp.bfloat16)
+        wide_sum[...] += outer(mix, grad)
+        bias_sum[...] += jnp.sum(grad, axis=0, keepdims=True)
         return carry
 
     lax.fori_loop(0, long // DENSE, step, 0)
+    stores = fetch([(grad_mixed_buf, grad_mixed)], sems.at[pl.ds(12, 1)])
     size = CHUNK // groups
 
     def store(i, carry):
@@ -393,111 +421,84 @@
         return carry
 
     lax.fori_loop(0, long // CHUNK, store, 0)
-    stores = fetch(
-        [(state_buf, state), (grad_mixed_buf, grad_mixed), (mixed_buf, mixed), (grad_buf, grad)],
-        sems.at[pl.ds(10, 4)],
-    )
-    walk(
-        groups, tail[1], tail[3], target, source, rel, window.at[pl.ds(long, long), :], table_buf, sums,
-    )
-
-    for k, (buf, out) in enumerate(((left_out, to_left), (right_out, to_right))):
-
-        def total(i, carry):
-            at = pl.multiple_of(i * CHUNK, CHUNK)
-            buf[pl.ds(at, CHUNK), :] = total_of(sums, k * long + at).astype(jnp.bfloat16)
-            return carry
-
-        lax.fori_loop(0, long // CHUNK, total, 0)
-        stores += fetch([(buf, out)], sems.at[pl.ds(14 + k, 1)])
+    stores += fetch([(state_buf, state)], sems.at[pl.ds(13, 1)])
+    weight_sum[...] = quarters(wide_sum[...])
     wait(stores)
 
 
+def folded(wide):
+    value = wide[:DIM, :DIM]
+    for g in range(1, LANES // DIM):
+        value = value + wide[g * DIM : (g + 1) * DIM, g * DIM : (g + 1) * DIM]
+    return value
+
+
+def folded_row(wide):
+    value = wide[:, :DIM]
+    for g in range(1, LANES // DIM):
+        value = value + wide[:, g * DIM : (g + 1) * DIM]
+    return value
+
+
 def adjoint_kernel(
-    groups, flat, grad_mixed, tables, cotangent, mixed, grad,
-    base, to_mirror, weight_sum, bias_sum,
-    source, target, rel, tail, grad_mixed_buf, table_buf, cotangent_buf, mixed_buf, grad_buf,
-    mirror_out, window, wide_sum, sems, *sums,
+    groups, weights, biases, weight_one, bias_one, flat, grad_mixed, tables, cotangent, own, mirror, left,
+    right, out,
+    source, target, rel, tail, grad_mixed_buf, table_buf, cotangent_buf, own_buf, mirror_buf, left_buf,
+    right_buf, window, wide_sum, bias_sum, sems, *sums,
 ):
     long = window.shape[0]
     lists = fetch_lists(flat, (source, target, rel, tail), tables, 1, table_buf, sems)
     loads = fetch([(grad_mixed, grad_mixed_buf)], sems.at[pl.ds(5, 1)])
     clear(sums)
+    wide_sum[...] = jnp.zeros_like(wide_sum)
+    bias_sum[...] = jnp.zeros_like(bias_sum)
+    wide = split(weights[0])
+    bias = biases[0]
     wait(loads)
     spread(grad_mixed_buf, window, 0)
     wait(lists)
     late = fetch(
-        [(cotangent, cotangent_buf), (mixed, mixed_buf), (grad, grad_buf)], sems.at[pl.ds(6, 3)]
-    )
+        [(left, left_buf), (right, right_buf), (mirror, mirror_buf), (own, own_buf)]
+        + [(cotangent, cotangent_buf)],
+        sems.at[pl.ds(6, 5)],
+    )
+
+    def add_products(mixed_buf, first, extra, again):
+        def step(i, carry):
+            at = pl.multiple_of(i * DENSE, DENSE)
+            terms = total_of(sums, first + at, DENSE)
+            if extra is not None:
+                terms = terms + extra[pl.ds(at, DENSE), :]
+            if again:
+                for ref in sums:
+                    ref[pl.ds(first + at, DENSE), :] = jnp.zeros((DENSE, LANES), jnp.float32)
+            mixed = mixed_buf[pl.ds(at, DENSE), :]
+            grad = terms * silu_slope(update_of(mixed, wide, bias))
+            wide_sum[...] += lax.dot_general(
+                mixed, split(grad), (((0,), (0,)), ((), ())), preferred_element_type=jnp.float32
+            )
+            bias_sum[...] += jnp.sum(grad, axis=0, keepdims=True)
+            return carry
+
+        lax.fori_loop(0, long // DENSE, step, 0)
+
+    walk(groups, tail[1], tail[3], target, source, rel, window, table_buf, sums)
+    wait(late)
+    add_products(left_buf, 0, None, True)
+    add_products(right_buf, long, None, True)
     walk(groups, 0, tail[1], target, source, rel, window, table_buf, sums)
-
-    def total(i, carry):
-        at = pl.multiple_of(i * CHUNK, CHUNK)
-        mirror_out[pl.ds(at, CHUNK), :] = total_of(sums, long + at).astype(jnp.bfloat16)
-        return carry
-
-    lax.fori_loop(0, long // CHUNK, total, 0)
-    stores = fetch([(mirror_out, to_mirror)], sems.at[pl.ds(9, 1)])
-    wait(late)
+    add_products(mirror_buf, long, None, False)
     spread(cotangent_buf, window, 0)
-    wide_sum[...] = jnp.zeros_like(wide_sum)
-    bias_sum[...] = jnp.zeros_like(bias_sum)
-
-    def step(i, carry):
-        at = pl.multiple_of(i * DENSE, DENSE)
-        rows = pl.ds(at, DENSE)
-        window[rows, :] += total_of(sums, at, DENSE)
-        values = grad_buf[rows, :]
-        wide_sum[...] += outer(mixed_buf[rows, :], values)
-        bias_sum[...] += jnp.sum(values, axis=0, keepdims=True)
-        return carry
-
-    lax.fori_loop(0, long // DENSE, step, 0)
-    stores += fetch([(window, base)], sems.at[pl.ds(10, 1)])
-    weight_sum[...] = quarters(wide_sum[...])
-    wait(stores)
+    add_products(own_buf, 0, window, False)
+    out[...] = jnp.zeros_like(out)
+    out[0:DIM, 0:DIM] = folded(wide_sum[:, :LANES] + wide_sum[:, LANES:])
+    out[DIM : 2 * DIM, 0:DIM] = folded(weight_one[...])
+    out[2 * DIM : 2 * DIM + 1, 0:DIM] = folded_row(bias_sum[...])
+    out[2 * DIM + 1 : 2 * DIM + 2, 0:DIM] = folded_row(bias_one[...])
 
 
 def copy_kernel(source, out, sems):
     wait(fetch([(source, out)], sems))
-
-
-def folded(wide):
-    value = wide[:DIM, :DIM]
-    for g in range(1, LANES // DIM):
-        value = value + wide[g * DIM : (g + 1) * DIM, g * DIM : (g + 1) * DIM]
-    return value
-
-
-def folded_row(wide):
-    value = wide[:, :DIM]
-    for g in range(1, LANES // DIM):
-        value = value + wide[:, g * DIM : (g + 1) * DIM]
-    return value
-
-
-def last_kernel(
-    base, left, right, mirror, update, mixed, weight_one, bias_one, out, wide_sum, bias_sum
-):
-    @pl.when(pl.program_id(0) == 0)
-    def _():
-        wide_sum[...] = jnp.zeros_like(wide_sum)
-        bias_sum[...] = jnp.zeros_like(bias_sum)
-
-    state_grad = base[...]
-    for ref in (left, right, mirror):
-        state_grad = state_grad + ref[...].astype(jnp.float32)
-    grad = state_grad * silu_slope(update[...])
-    wide_sum[...] += outer(mixed[...], grad)
-    bias_sum[...] += jnp.sum(grad, axis=0, keepdims=True)
-
-    @pl.when(pl.program_id(0) == pl.num_programs(0) - 1)
-    def _():
-        out[...] = jnp.zeros_like(out)
-        out[0:DIM, 0:DIM] = folded(quarters(wide_sum[...]))
-        out[DIM : 2 * DIM, 0:DIM] = folded(weight_one[...])
-        out[2 * DIM : 2 * DIM + 1, 0:DIM] = folded_row(bias_sum[...])
-        out[2 * DIM + 1 : 2 * DIM + 2, 0:DIM] = folded_row(bias_one[...])
 
 
 def edge_lists(edge_tiles, row_count, groups, rel_count):
@@ -511,7 +512,9 @@
         functools.partial(
             bucket_kernel, tile_count=tile_count, row_count=row_count, rel_count=rel_count
         ),
-        out_shape=[jax.ShapeDtypeStruct((room,), jnp.int32), jax.ShapeDtypeStruct((4,), jnp.int32)],
+        out_shape=[
+            jax.ShapeDtypeStruct((room,), jnp.int32), jax.ShapeDtypeStruct((4,), jnp.int32)
+        ],
         in_specs=[VMEM],
         out_specs=[SMEM] * 2,
         scratch_shapes=[flat] * 5
@@ -546,9 +549,7 @@
         return lax.ppermute(block, AXES, route)
 
     def run(fn, args, specs, outs, out_specs, scratch):
-        return pl.pallas_call(
-            fn, out_shape=outs, in_specs=specs, out_specs=out_specs, scratch_shapes=scratch,
-        )(*args)
+        return pl.pallas_call(fn, out_shape=outs, in_specs=specs, out_specs=out_specs, scratch_shapes=scratch)(*args)
 
     wide_f32 = jax.ShapeDtypeStruct((long, LANES), jnp.float32)
     wide_bf16 = jax.ShapeDtypeStruct((long, LANES), jnp.bfloat16)
@@ -595,74 +596,64 @@
     def sems(count):
         return pltpu.SemaphoreType.DMA((count,))
 
-    def halo(state, index):
-        buf = pltpu.VMEM(state.shape, jnp.bfloat16)
-        mirror = send(state, seats.mirror())
-        left = send(state, seats.shift(1))
-        right = send(state, seats.shift(-1))
-        near = run(
-            functools.partial(near_kernel, groups, index),
-            [flat, state, mirror, tables],
-            [ANY] * 4,
-            wide_f32,
-            ANY,
-            [*list_bufs, buf, buf, table_buf, pair, sems(11), *sums],
-        )
-        return left, right, near
-
-    left, right, near = halo(state_zero, 0)
+    def halo(block):
+        mirror = send(block, seats.mirror())
+        left = send(block, seats.shift(1))
+        right = send(block, seats.shift(-1))
+        return mirror, left, right
+
     block_buf = pltpu.VMEM(state_zero.shape, jnp.bfloat16)
-    state_one, mixed_zero, update_zero = run(
+    mirror, left, right = halo(state_zero)
+    near = run(
+        functools.partial(near_zero_kernel, groups),
+        [flat, state_zero, mirror, tables],
+        [ANY] * 4,
+        wide_f32,
+        ANY,
+        [*list_bufs, block_buf, block_buf, table_buf, pair, sems(11), *sums],
+    )
+    state_one, mixed = run(
         functools.partial(first_kernel, groups),
         [head_rows, weights, biases, flat, left, right, near, tables, state_zero],
         [VMEM] * 3 + [ANY] * 6,
-        [wide_bf16, wide_f32, wide_f32],
-        [ANY] * 3,
-        [*list_bufs, block_buf, block_buf, table_buf, block_buf, pair, f32_buf, f32_buf, bf16_buf, sems(21)]
-        + sums,
-    )
-    left, right, near = halo(state_one, 1)
-    state_two, grad_mixed, mixed_one, grad_one, to_left, to_right = run(
+        [wide_bf16, wide_bf16],
+        [ANY] * 2,
+        [*list_bufs, block_buf, block_buf, table_buf, block_buf, pair, bf16_buf, bf16_buf, sems(17), *sums],
+    )
+    mirror_mixed, left_mixed, right_mixed = halo(mixed)
+    near = run(
+        functools.partial(near_one_kernel, groups),
+        [weights, biases, flat, state_one, mirror, mirror_mixed, tables],
+        [VMEM] * 2 + [ANY] * 5,
+        wide_f32,
+        ANY,
+        [*list_bufs, bf16_buf, block_buf, bf16_buf, table_buf, pair, sems(12), *sums],
+    )
+    state_two, grad_mixed, weight_one, bias_one = run(
         functools.partial(second_kernel, groups),
-        [head_rows, weights, biases, flat, left, right, near, tables, state_one, grad_out],
-        [VMEM] * 3 + [ANY] * 7,
-        [jax.ShapeDtypeStruct(entity_state.shape, jnp.bfloat16), wide_bf16, wide_f32, wide_f32]
-        + [wide_bf16] * 2,
-        [ANY] * 6,
-        [*list_bufs, bf16_buf, bf16_buf, table_buf, bf16_buf, block_buf, pair, f32_buf, f32_buf, bf16_buf]
-        + [block_buf, bf16_buf, bf16_buf, sems(16), *pair_sums],
-    )
-    from_right = send(to_left, seats.shift(-1))
-    from_left = send(to_right, seats.shift(1))
+        [head_rows, weights, biases, flat, left, right, left_mixed, right_mixed, near, tables, state_one]
+        + [grad_out],
+        [VMEM] * 3 + [ANY] * 9,
+        [jax.ShapeDtypeStruct(entity_state.shape, jnp.bfloat16), wide_bf16, square, line],
+        [ANY] * 2 + [VMEM] * 2,
+        [*list_bufs, block_buf, block_buf, bf16_buf, bf16_buf, table_buf, bf16_buf, block_buf, pair]
+        + [bf16_buf, block_buf, pltpu.VMEM((2 * LANES, 2 * LANES), jnp.float32), sems(14), *sums],
+    )
     final_state = run(
         copy_kernel, [send(state_two, seats.give_back())], [ANY],
         jax.ShapeDtypeStruct(entity_state.shape, jnp.bfloat16), VMEM, [sems(1)],
     )
-    base, to_mirror, weight_one, bias_one = run(
+    grads = run(
         functools.partial(adjoint_kernel, groups),
-        [flat, grad_mixed, tables, grad_out, mixed_one, grad_one],
-        [ANY] * 6,
-        [wide_f32, wide_bf16, square, line],
-        [ANY] * 2 + [VMEM] * 2,
-        [*list_bufs, bf16_buf, table_buf, block_buf, f32_buf, f32_buf, bf16_buf, f32_buf]
-        + [pltpu.VMEM((2 * LANES, 2 * LANES), jnp.float32), sems(11), *pair_sums],
-    )
-    from_mirror = send(to_mirror, seats.mirror())
-    steps = 4
-    rows = pl.BlockSpec((long // steps, LANES), lambda i: (i, 0))
-    whole = lambda shape: pl.BlockSpec(shape, lambda i: (0, 0))
-    grads = pl.pallas_call(
-        last_kernel,
-        out_shape=jax.ShapeDtypeStruct((2 * DIM + 8, LANES), jnp.float32),
-        grid=(steps,),
-        in_specs=[rows] * 6 + [whole((LANES, LANES)), whole((1, LANES))],
-        out_specs=whole((2 * DIM + 8, LANES)),
-        scratch_shapes=[
-            pltpu.VMEM((2 * LANES, 2 * LANES), jnp.float32),
-            pltpu.VMEM((1, LANES), jnp.float32),
-        ],
-        name="last",
-    )(base, from_left, from_right, from_mirror, update_zero, mixed_zero, weight_one, bias_one)
+        [weights, biases, weight_one, bias_one, flat, grad_mixed, tables, grad_out, mixed, mirror_mixed]
+        + [left_mixed, right_mixed],
+        [VMEM] * 4 + [ANY] * 8,
+        jax.ShapeDtypeStruct((2 * DIM + 8, LANES), jnp.float32),
+        VMEM,
+        [*list_bufs, bf16_buf, table_buf, block_buf, bf16_buf, bf16_buf, bf16_buf, bf16_buf, f32_buf]
+        + [pltpu.VMEM((LANES, 2 * LANES), jnp.float32), pltpu.VMEM((1, LANES), jnp.float32), sems(11)]
+        + pair_sums,
+    )
     devices = seats.nodes * seats.queries
     reach = 1
     while reach < devices:
@@ -686,6 +677,4 @@
         P("node", "query"),
     )
 
-    return jax.shard_map(
-        body, mesh=mesh, in_specs=placed, out_specs=(P("node", "query"), P(), P()), check_vma=False
-    )
+    return jax.shard_map(body, mesh=mesh, in_specs=placed, out_specs=(P("node", "query"), P(), P()), check_vma=False)

time: 208 us -> 209 us (level)
  waiting for transfers between devices: 59.6 us -> 48.7 us
  Pallas kernels: 106 us -> 116 us
  local copies, waits for them, and re-layouts: 9.59 us -> 15 us
  starting transfers between devices: 23.2 us -> 19.5 us
    pallas_call x6, Pallas kernels: 82.1 us -> 98.4 us  [run(): pl.pallas_call(fn, out_shape=outs, in_specs=specs, out_specs=out_specs, s...]
    ppermute x18 -> x15, waiting for transfers between devices: 59.6 us -> 48.7 us  [send(): return lax.ppermute(block, AXES, route)]
    pallas_call x1 -> x0, Pallas kernels: 6.05 us -> none  [body(): pl.pallas_call(last_kernel, out_shape=jax.ShapeDtypeStruct((2 * DIM + 8,...]
    ppermute x18 -> x15, starting transfers between devices: 23.2 us -> 19.5 us  [send(): return lax.ppermute(block, AXES, route)]
    another operation x2, local copies, waits for them, and re-layouts: 1.28 us -> 3.39 us  [body(): jnp.tile(jnp.pad(rel_vectors, ((0, 0), (0, -rel_count % 8 or 8), (0, 0)))...]
    unnamed x22 -> x18, local copies, waits for them, and re-layouts: 4.54 us -> 5.03 us
  transfers between devices with their start and end apart: 18 -> 15, of which waited for: 9 -> 9; matrix products, arithmetic and copies ran while one was open for 4% -> 7% of each run, Pallas kernels for 32% -> 38%
where the time goes in v1:
time: 209 us; the launch traced here: 206 us
  Pallas kernels  116 us (56%)
  waiting for transfers between devices  48.7 us (23%)
  starting transfers between devices  19.5 us (9%)
  local copies, waits for them, and re-layouts  15 us (7%)
  other arithmetic  5.07 us (2%)
    pallas_call x6, Pallas kernels, run(): pl.pallas_call(fn, out_shape=outs, in_specs=specs, out_specs=out_specs, s...  98.4 us
    ppermute x15, waiting for transfers between devices, send(): return lax.ppermute(block, AXES, route)  48.7 us
    ppermute x15, starting transfers between devices, send(): return lax.ppermute(block, AXES, route)  19.5 us
    pallas_call x1, Pallas kernels, edge_lists(): pl.pallas_call(functools.partial(bucket_kernel, tile_count=tile_count, ro...  17.9 us
    unnamed x18, local copies, waits for them, and re-layouts  5.03 us
  transfers between devices with their start and end apart: 15, of which 9 were waited for; matrix products, arithmetic and copies ran while one was open for 7% of the time, Pallas kernels for 38%

profile of v1, /device:TPU:10, one launch (start us, length us, event | category | flops | bytes accessed | tf_op | source)
XLA Modules:
  0.0 205.6 jit_solution(274297943941281544)
XLA Ops:
  0.6 2.6 %collective-permute-start.1 = (bf16[1024,512]{1,0:T(8,128)(2,1)}, bf16[1024,512]{1,0:T(8,128)(2,1)S(1)}, u32[]{:S(2)}, u32[]{:S(2)}) collective-permute-start(bf16[1024,512]{1,0:T(8,128)(2,1)} %param.9), channel_id=1, source_target_pairs={{0,0},{1,16},{2,2},{3,18},{4,4},{5,20},{6,6},{7,22},{8,12},{9,28},... | collective-permute-start | bytes 3145736 | tf_op jit(solution)/shard_map/ppermute | solution.py:549
  3.9 17.9 %bucket.1 = (s32[9216]{0:T(1024)}, s32[4]{0:T(128)}) custom-call(s32[3,16,512]{2,1,0:T(8,128)} %bitcast.5), custom_call_target="tpu_custom_call" | custom-call | tf_op jit(solution)/shard_map/bucket/pallas_call | solution.py:511
  24.0 3.4 %collective-permute-start = (s32[28672]{0:T(1024)}, s32[28672]{0:T(1024)S(1)}, u32[]{:S(2)}, u32[]{:S(2)}) collective-permute-start(s32[28672]{0:T(1024)} %pad_add_fusion), channel_id=1, source_target_pairs={{0,0},{1,16},{2,2},{3,18},{4,4},{5,20},{6,6},{7,22},{8,12},{9,28},... | collective-permute-start | bytes 344072 | tf_op jit(solution)/shard_map/ppermute | solution.py:549
  27.4 1.5 collective-permute-done.1.own
  31.1 1.6 tile.18
  38.1 2.4 %copy.13.tables = f32[2,824,128]{2,1,0:T(8,128)} copy(f32[2,824,128]{1,2,0:T(8,128)} %bitcast.4) | data formatting | bytes 1687552 | tf_op jit(solution)/shard_map/tile | solution.py:589
  41.6 11.9 %shard_map.112.near = f32[4096,128]{1,0:T(8,128)} custom-call(s32[28672]{0:T(1024)} %copy-done.7, bf16[1024,512]{1,0:T(8,128)(2,1)} %copy-done.1, bf16[1024,512]{1,0:T(8,128)(2,1)} %collective-permute-done.4.mirror, f32[2,824,128]{2,1,0:T(8,128)} %copy.13.tables), custom_call_target="tpu_custom_call" | custom-call | tf_op jit(solution)/shard_map/pallas_call | solution.py:552
  53.5 2.2 %collective-permute-done.3.right = bf16[1024,512]{1,0:T(8,128)(2,1)S(1)} collective-permute-done((bf16[1024,512]{1,0:T(8,128)(2,1)S(1)}, bf16[1024,512]{1,0:T(8,128)(2,1)S(1)}, u32[]{:S(2)}, u32[]{:S(2)}) %collective-permute-start.3) | collective-permute-done | bytes 1048608 | tf_op jit(solution)/shard_map/ppermute | solution.py:549
  57.7 14.5 %shard_map.113 = (bf16[4096,128]{1,0:T(8,128)(2,1)}, bf16[4096,128]{1,0:T(8,128)(2,1)}) custom-call(f32[16,128]{1,0:T(8,128)} %compare_select_fusion.head_rows, f32[2,128,128]{2,1,0:T(8,128)} %broadcast_select_fusion.weights, f32[2,1,128]{2,1,0:T(1,128)} %tile.40.biases, s32[28672]{0:T(1024)} %copy-done.7, bf16[1024,512]{1,0:T(8,128)(2,1)} %copy-done.3, ...), custom_call_target="tpu_custom_call" | custom-call | tf_op jit(solution)/shard_map/pallas_call | solution.py:552
  72.3 2.7 %collective-permute-start.8 = (bf16[1024,512]{1,0:T(8,128)(2,1)}, bf16[1024,512]{1,0:T(8,128)(2,1)S(1)}, u32[]{:S(2)}, u32[]{:S(2)}) collective-permute-start(bf16[1024,512]{1,0:T(8,128)(2,1)} %param.17), channel_id=1, source_target_pairs={{0,0},{1,16},{2,2},{3,18},{4,4},{5,20},{6,6},{7,22},{8,12},{9,28},... | collective-permute-start | bytes 3145736 | tf_op jit(solution)/shard_map/ppermute | solution.py:549
  75.1 2.0 collective-permute-start.5
  77.1 14.5 %shard_map.114.near = f32[4096,128]{1,0:T(8,128)} custom-call(f32[2,128,128]{2,1,0:T(8,128)} %broadcast_select_fusion.weights, f32[2,1,128]{2,1,0:T(1,128)} %tile.40.biases, s32[28672]{0:T(1024)} %copy-done.7, bf16[4096,128]{1,0:T(8,128)(2,1)} %get-tuple-element.14.own, bf16[1024,512]{1,0:T(8,128)(2,1)} %collective-permute-done.4.mirror, ...), custom_call_target="tpu_custom_call" | custom-call | tf_op jit(solution)/shard_map/pallas_call | solution.py:552
  91.6 18.0 %collective-permute-done.8.cotangent = bf16[1024,512]{1,0:T(8,128)(2,1)S(1)} collective-permute-done((bf16[1024,512]{1,0:T(8,128)(2,1)}, bf16[1024,512]{1,0:T(8,128)(2,1)S(1)}, u32[]{:S(2)}, u32[]{:S(2)}) %collective-permute-start.8) | collective-permute-done | bytes 1048608 | tf_op jit(solution)/shard_map/ppermute | solution.py:549
  109.6 13.2 %collective-permute-done.6.right_mixed.right = bf16[4096,128]{1,0:T(8,128)(2,1)S(1)} collective-permute-done((bf16[4096,128]{1,0:T(8,128)(2,1)}, bf16[4096,128]{1,0:T(8,128)(2,1)S(1)}, u32[]{:S(2)}, u32[]{:S(2)}) %collective-permute-start.6) | collective-permute-done | bytes 1048608 | tf_op jit(solution)/shard_map/ppermute | solution.py:549
  124.9 21.0 %shard_map.115 = (bf16[1024,512]{1,0:T(8,128)(2,1)}, bf16[4096,128]{1,0:T(8,128)(2,1)}, f32[128,128]{1,0:T(8,128)}, f32[1,128]{1,0:T(1,128)}) custom-call(f32[16,128]{1,0:T(8,128)} %compare_select_fusion.head_rows, f32[2,128,128]{2,1,0:T(8,128)} %broadcast_select_fusion.weights, f32[2,1,128]{2,1,0:T(1,128)} %tile.40.biases, s32[28672]{0:T(1024)} %copy-done.7, ...), custom_call_target="tpu_custom_call" | custom-call | tf_op jit(solution)/shard_map/pallas_call | solution.py:552
  145.9 1.9 collective-permute-start.9
  147.9 34.3 %shard_map.117 = f32[72,128]{1,0:T(8,128)} custom-call(f32[2,128,128]{2,1,0:T(8,128)} %broadcast_select_fusion.weights, f32[2,1,128]{2,1,0:T(1,128)} %tile.40.biases, f32[128,128]{1,0:T(8,128)} %get-tuple-element.16.weight_one, f32[1,128]{1,0:T(1,128)} %get-tuple-element.17.bias_one, s32[28672]{0:T(1024)} %copy-done.7, ...), custom_call_target="tpu_custom_call" | custom-call | tf_op jit(solution)/shard_map/pallas_call | solution.py:552
  184.4 1.5 collective-permute-start.11
  185.9 2.4 %collective-permute-done.11 = f32[72,128]{1,0:T(8,128)S(1)} collective-permute-done((f32[72,128]{1,0:T(8,128)S(1)}, f32[72,128]{1,0:T(8,128)S(1)}, u32[]{:S(2)}, u32[]{:S(2)}) %collective-permute-start.11) | collective-permute-done | bytes 36896 | tf_op jit(solution)/shard_map/ppermute | solution.py:549
  188.4 2.0 collective-permute-start.12
  190.4 1.9 collective-permute-done.12
  192.4 3.9 %collective-permute-done.13 = f32[72,128]{1,0:T(8,128)S(1)} collective-permute-done((f32[72,128]{1,0:T(8,128)S(1)}, f32[72,128]{1,0:T(8,128)S(1)}, u32[]{:S(2)}, u32[]{:S(2)}) %collective-permute-start.13) | collective-permute-done | bytes 36896 | tf_op jit(solution)/shard_map/ppermute | solution.py:549
  197.3 3.9 %collective-permute-done.14 = f32[72,128]{1,0:T(8,128)S(1)} collective-permute-done((f32[72,128]{1,0:T(8,128)S(1)}, f32[72,128]{1,0:T(8,128)S(1)}, u32[]{:S(2)}, u32[]{:S(2)}) %collective-permute-start.14) | collective-permute-done | bytes 36896 | tf_op jit(solution)/shard_map/ppermute | solution.py:549
  203.4 2.2 %shard_map.116 = bf16[1024,512]{1,0:T(8,128)(2,1)} custom-call(bf16[1024,512]{1,0:T(8,128)(2,1)} %copy-done.8), custom_call_target="tpu_custom_call" | custom-call | tf_op jit(solution)/shard_map/pallas_call | solution.py:552
  (58 shorter events, 21.0 us)
Async XLA Ops:
  0.6 39.9 %copy-start = (f32[822,32]{0,1:T(8,128)S(1)}, f32[822,32]{0,1:T(8,128)}, u32[]{:S(2)}) copy-start(f32[822,32]{0,1:T(8,128)} %param.13) | copy-start | bytes 315652
  0.6 28.3 %collective-permute-start.1 = (bf16[1024,512]{1,0:T(8,128)(2,1)}, bf16[1024,512]{1,0:T(8,128)(2,1)S(1)}, u32[]{:S(2)}, u32[]{:S(2)}) collective-permute-start(bf16[1024,512]{1,0:T(8,128)(2,1)} %param.9), channel_id=1, source_target_pairs={{0,0},{1,16},{2,2},{3,18},{4,4},{5,20},{6,6},{7,22},{8,12},{9,28},... | collective-permute-start | bytes 3145736 | tf_op jit(solution)/shard_map/ppermute | solution.py:549
  24.0 16.5 %collective-permute-start = (s32[28672]{0:T(1024)}, s32[28672]{0:T(1024)S(1)}, u32[]{:S(2)}, u32[]{:S(2)}) collective-permute-start(s32[28672]{0:T(1024)} %pad_add_fusion), channel_id=1, source_target_pairs={{0,0},{1,16},{2,2},{3,18},{4,4},{5,20},{6,6},{7,22},{8,12},{9,28},... | collective-permute-start | bytes 344072 | tf_op jit(solution)/shard_map/ppermute | solution.py:549
  28.9 11.6 %copy-start.1 = (bf16[1024,512]{1,0:T(8,128)(2,1)}, bf16[1024,512]{1,0:T(8,128)(2,1)S(1)}, u32[]{:S(2)}) copy-start(bf16[1024,512]{1,0:T(8,128)(2,1)S(1)} %collective-permute-done.1.own) | copy-start | bytes 3145732
  28.9 12.7 %collective-permute-start.4 = (bf16[1024,512]{1,0:T(8,128)(2,1)S(1)}, bf16[1024,512]{1,0:T(8,128)(2,1)}, u32[]{:S(2)}, u32[]{:S(2)}) collective-permute-start(bf16[1024,512]{1,0:T(8,128)(2,1)S(1)} %collective-permute-done.1.own), channel_id=1, source_target_pairs={{0,1},{16,17},{2,3},{18,19},{4,5},{20,21},{6,7},{22,23},{12,13},{2... | collective-permute-start | bytes 3145736 | tf_op jit(solution)/shard_map/ppermute | solution.py:549
  29.1 26.6 %collective-permute-start.3 = (bf16[1024,512]{1,0:T(8,128)(2,1)S(1)}, bf16[1024,512]{1,0:T(8,128)(2,1)S(1)}, u32[]{:S(2)}, u32[]{:S(2)}) collective-permute-start(bf16[1024,512]{1,0:T(8,128)(2,1)S(1)} %collective-permute-done.1.own), channel_id=1, source_target_pairs={{4,0},{20,16},{6,2},{22,18},{12,4},{28,20},{14,6},{30,22},{8,12},{... | collective-permute-start | bytes 3145736 | tf_op jit(solution)/shard_map/ppermute | solution.py:549
  29.8 26.0 %collective-permute-start.2 = (bf16[1024,512]{1,0:T(8,128)(2,1)S(1)}, bf16[1024,512]{1,0:T(8,128)(2,1)S(1)}, u32[]{:S(2)}, u32[]{:S(2)}) collective-permute-start(bf16[1024,512]{1,0:T(8,128)(2,1)S(1)} %collective-permute-done.1.own), channel_id=1, source_target_pairs={{9,0},{25,16},{11,2},{27,18},{0,4},{16,20},{2,6},{18,22},{4,12},{2... | collective-permute-start | bytes 3145736 | tf_op jit(solution)/shard_map/ppermute | solution.py:549
  40.5 1.1 copy-start.7
  55.7 1.0 copy-start.2
  56.7 1.0 copy-start.3
  72.2 4.9 %collective-permute-start.7 = (bf16[4096,128]{1,0:T(8,128)(2,1)}, bf16[4096,128]{1,0:T(8,128)(2,1)}, u32[]{:S(2)}, u32[]{:S(2)}) collective-permute-start(bf16[4096,128]{1,0:T(8,128)(2,1)} %get-tuple-element.13.own), channel_id=1, source_target_pairs={{0,1},{16,17},{2,3},{18,19},{4,5},{20,21},{6,7},{22,23},{12,13},{2... | collective-permute-start | bytes 3145736 | tf_op jit(solution)/shard_map/ppermute | solution.py:549
  72.3 37.4 %collective-permute-start.8 = (bf16[1024,512]{1,0:T(8,128)(2,1)}, bf16[1024,512]{1,0:T(8,128)(2,1)S(1)}, u32[]{:S(2)}, u32[]{:S(2)}) collective-permute-start(bf16[1024,512]{1,0:T(8,128)(2,1)} %param.17), channel_id=1, source_target_pairs={{0,0},{1,16},{2,2},{3,18},{4,4},{5,20},{6,6},{7,22},{8,12},{9,28},... | collective-permute-start | bytes 3145736 | tf_op jit(solution)/shard_map/ppermute | solution.py:549
  75.0 47.9 %collective-permute-start.6 = (bf16[4096,128]{1,0:T(8,128)(2,1)}, bf16[4096,128]{1,0:T(8,128)(2,1)S(1)}, u32[]{:S(2)}, u32[]{:S(2)}) collective-permute-start(bf16[4096,128]{1,0:T(8,128)(2,1)} %get-tuple-element.13.own), channel_id=1, source_target_pairs={{4,0},{20,16},{6,2},{22,18},{12,4},{28,20},{14,6},{30,22},{8,12},{... | collective-permute-start | bytes 3145736 | tf_op jit(solution)/shard_map/ppermute | solution.py:549
  75.1 47.8 %collective-permute-start.5 = (bf16[4096,128]{1,0:T(8,128)(2,1)}, bf16[4096,128]{1,0:T(8,128)(2,1)S(1)}, u32[]{:S(2)}, u32[]{:S(2)}) collective-permute-start(bf16[4096,128]{1,0:T(8,128)(2,1)} %get-tuple-element.13.own), channel_id=1, source_target_pairs={{9,0},{25,16},{11,2},{27,18},{0,4},{16,20},{2,6},{18,22},{4,12},{2... | collective-permute-start | bytes 3145736 | tf_op jit(solution)/shard_map/ppermute | solution.py:549
  109.6 13.2 %copy-start.4 = (bf16[1024,512]{1,0:T(8,128)(2,1)}, bf16[1024,512]{1,0:T(8,128)(2,1)S(1)}, u32[]{:S(2)}) copy-start(bf16[1024,512]{1,0:T(8,128)(2,1)S(1)} %collective-permute-done.8.cotangent) | copy-start | bytes 3145732
  122.9 1.1 copy-start.5
  123.9 1.0 copy-start.6
  145.9 56.4 %collective-permute-start.9 = (bf16[1024,512]{1,0:T(8,128)(2,1)}, bf16[1024,512]{1,0:T(8,128)(2,1)S(1)}, u32[]{:S(2)}, u32[]{:S(2)}) collective-permute-start(bf16[1024,512]{1,0:T(8,128)(2,1)} %get-tuple-element.15), channel_id=1, source_target_pairs={{0,0},{16,1},{2,2},{18,3},{4,4},{20,5},{6,6},{22,7},{12,8},{28,9},... | collective-permute-start | bytes 3145736 | tf_op jit(solution)/shard_map/ppermute | solution.py:549
  182.1 1.5 collective-permute-start.10
  184.4 4.0 %collective-permute-start.11 = (f32[72,128]{1,0:T(8,128)S(1)}, f32[72,128]{1,0:T(8,128)S(1)}, u32[]{:S(2)}, u32[]{:S(2)}) collective-permute-start(f32[72,128]{1,0:T(8,128)S(1)} %add.39), channel_id=1, source_target_pairs={{0,2},{1,3},{2,0},{3,1},{4,6},{5,7},{6,4},{7,5},{8,10},{9,11},{10,... | collective-permute-start | bytes 110600 | tf_op jit(solution)/shard_map/ppermute | solution.py:549
  188.4 4.0 %collective-permute-start.12 = (f32[72,128]{1,0:T(8,128)S(1)}, f32[72,128]{1,0:T(8,128)S(1)}, u32[]{:S(2)}, u32[]{:S(2)}) collective-permute-start(f32[72,128]{1,0:T(8,128)S(1)} %add.40), channel_id=1, source_target_pairs={{0,4},{1,5},{2,6},{3,7},{4,0},{5,1},{6,2},{7,3},{8,12},{9,13},{10,... | collective-permute-start | bytes 110600 | tf_op jit(solution)/shard_map/ppermute | solution.py:549
  192.4 4.0 %collective-permute-start.13 = (f32[72,128]{1,0:T(8,128)S(1)}, f32[72,128]{1,0:T(8,128)S(1)}, u32[]{:S(2)}, u32[]{:S(2)}) collective-permute-start(f32[72,128]{1,0:T(8,128)S(1)} %add.41), channel_id=1, source_target_pairs={{0,8},{1,9},{2,10},{3,11},{4,12},{5,13},{6,14},{7,15},{8,0},{9,1},... | collective-permute-start | bytes 110600 | tf_op jit(solution)/shard_map/ppermute | solution.py:549
  196.3 4.9 %collective-permute-start.14 = (f32[72,128]{1,0:T(8,128)S(1)}, f32[72,128]{1,0:T(8,128)S(1)}, u32[]{:S(2)}, u32[]{:S(2)}) collective-permute-start(f32[72,128]{1,0:T(8,128)S(1)} %add.42), channel_id=1, source_target_pairs={{0,16},{1,17},{2,18},{3,19},{4,20},{5,21},{6,22},{7,23},{8,24},{9,... | collective-permute-start | bytes 110600 | tf_op jit(solution)/shard_map/ppermute | solution.py:549
  202.4 1.0 copy-start.8

commit v2 on v1

--- a/solution.py
+++ b/solution.py
@@ -13,18 +13,13 @@
 UNROLL = 48
 SUMS = 3
 CHUNK = 256
-DENSE = 512
+DENSE = 1024
 LINE = 1024
 AXES = ("node", "query")
 HIGHEST = lax.Precision.HIGHEST
 SMEM = pl.BlockSpec(memory_space=pltpu.SMEM)
 VMEM = pl.BlockSpec(memory_space=pltpu.VMEM)
 ANY = pl.BlockSpec(memory_space=pl.ANY)
-
-
-def silu_slope(values):
-    sigma = jax.nn.sigmoid(values)
-    return sigma * (1.0 + values * (1.0 - sigma))
 
 
 class Seats:
@@ -225,24 +220,59 @@
     )
 
 
+def outer_rounded(left, right):
+    return lax.dot_general(
+        left, split(right), (((0,), (0,)), ((), ())), preferred_element_type=jnp.float32
+    )
+
+
 def quarters(wide):
     return (
         wide[:LANES, :LANES] + wide[LANES:, :LANES] + wide[:LANES, LANES:] + wide[LANES:, LANES:]
     )
 
 
+def make_table(rels, index, table):
+    count = rels.shape[2]
+    for at in range(0, table.shape[0], LANES):
+        size = min(LANES, count - at)
+        piece = rels[index, :, at : at + size]
+        if size < LANES:
+            piece = jnp.concatenate([piece, jnp.zeros((DIM, LANES - size), jnp.float32)], axis=1)
+        table[at : at + LANES, :] = jnp.concatenate([piece] * (LANES // DIM), axis=0).T
+
+
+def block_weight(weight):
+    repeat = LANES // DIM
+    wide = jnp.concatenate([jnp.concatenate([weight] * repeat, axis=1)] * repeat, axis=0)
+    row = lax.broadcasted_iota(jnp.int32, wide.shape, 0)
+    lane = lax.broadcasted_iota(jnp.int32, wide.shape, 1)
+    return jnp.where((row & -DIM) == (lane & -DIM), wide, 0.0)
+
+
+def block_bias(bias):
+    return jnp.concatenate([bias] * (LANES // DIM), axis=1)
+
+
 def update_of(mixed, wide, bias):
     both = jnp.dot(mixed, wide, preferred_element_type=jnp.float32)
     return both[:, :LANES] + both[:, LANES:] + bias
 
 
-def advance(state_buf, mixed_buf, window, first, wide, bias):
+def slope_from(values, sigma):
+    return sigma * (1.0 + values * (1.0 - sigma))
+
+
+def advance(state_buf, mixed_buf, window, first, wide, bias, slope_buf=None):
     spread(state_buf, window, first)
 
     def step(i, carry):
         at = pl.multiple_of(i * DENSE, DENSE)
         values = update_of(mixed_buf[pl.ds(at, DENSE), :], wide, bias)
-        window[pl.ds(first + at, DENSE), :] += values * jax.nn.sigmoid(values)
+        sigma = jax.nn.sigmoid(values)
+        window[pl.ds(first + at, DENSE), :] += values * sigma
+        if slope_buf is not None:
+            slope_buf[pl.ds(at, DENSE), :] = slope_from(values, sigma)
         return carry
 
     lax.fori_loop(0, mixed_buf.shape[0] // DENSE, step, 0)
@@ -266,12 +296,13 @@
 
 
 def near_zero_kernel(
-    groups, flat, own, mirror, tables, out,
+    groups, rels, flat, own, mirror, out,
     source, target, rel, tail, own_buf, mirror_buf, table_buf, window, sems, *sums,
 ):
     long = sums[0].shape[0]
-    lists = fetch_lists(flat, (source, target, rel, tail), tables, 0, table_buf, sems)
+    lists = fetch_lists(flat, (source, target, rel, tail), sems)
     states = fetch([(own, own_buf), (mirror, mirror_buf)], sems.at[pl.ds(5, 2)])
+    make_table(rels, 0, table_buf)
     clear(sums)
     states[0].wait()
     spread(own_buf, window, 0)
@@ -283,18 +314,19 @@
 
 
 def near_one_kernel(
-    groups, weights, biases, flat, own, mirror, mirror_mixed, tables, out,
+    groups, rels, weights, biases, flat, own, mirror, mirror_mixed, out,
     source, target, rel, tail, own_buf, mirror_buf, mixed_buf, table_buf, window, sems, *sums,
 ):
     long = sums[0].shape[0]
-    lists = fetch_lists(flat, (source, target, rel, tail), tables, 1, table_buf, sems)
+    lists = fetch_lists(flat, (source, target, rel, tail), sems)
     states = fetch(
         [(own, own_buf), (mirror, mirror_buf), (mirror_mixed, mixed_buf)], sems.at[pl.ds(5, 3)]
     )
+    make_table(rels, 1, table_buf)
     clear(sums)
     wait(states)
     spread(own_buf, window, 0)
-    advance(mirror_buf, mixed_buf, window, long, split(weights[0]), biases[0])
+    advance(mirror_buf, mixed_buf, window, long, split(block_weight(weights[0])), block_bias(biases[0:1, :]))
     wait(lists)
     walk(groups, 0, tail[1], source, target, rel, window, table_buf, sums)
     send_total(sums, out, sems.at[pl.ds(8, 4)])
@@ -310,20 +342,21 @@
             ref[pl.ds(at, 1), :] += head_rows[q : q + 1, :]
 
 
-def fetch_lists(flat, bufs, tables, index, table_buf, sems):
+def fetch_lists(flat, bufs, sems):
     room = bufs[0].shape[0]
     pairs = [(flat.at[pl.ds(k * room, buf.shape[0])], buf) for k, buf in enumerate(bufs)]
-    return fetch(pairs + [(tables.at[index], table_buf)], sems)
+    return fetch(pairs, sems)
 
 
 def first_kernel(
-    groups, head_rows, weights, biases, flat, left, right, near, tables, own, state, mixed,
+    groups, rels, head_rows, weights, biases, flat, left, right, near, own, state, mixed,
     source, target, rel, tail, left_buf, right_buf, table_buf, own_buf, window, mixed_buf, state_buf,
     sems, *sums,
 ):
     long = sums[0].shape[0]
-    lists = fetch_lists(flat, (source, target, rel, tail), tables, 0, table_buf, sems)
+    lists = fetch_lists(flat, (source, target, rel, tail), sems)
     states = fetch([(left, left_buf), (right, right_buf), (near, sums[0])], sems.at[pl.ds(5, 3)])
+    make_table(rels, 0, table_buf)
     clear(sums[1:])
     states[0].wait()
     spread(left_buf, window, 0)
@@ -336,8 +369,8 @@
     walk(groups, tail[1], tail[3], source, target, rel, window, table_buf, sums)
     wait(extra)
     spread(own_buf, window, 0)
-    wide = split_weight(weights[0])
-    bias = biases[0]
+    wide = split_weight(block_weight(weights[0]))
+    bias = block_bias(biases[0:1, :])
     parts = 4
     size = long // parts
     stores = []
@@ -364,10 +397,10 @@
 
 
 def second_kernel(
-    groups, head_rows, weights, biases, flat, left, right, left_mixed, right_mixed, near, tables, own,
-    cotangent, state, grad_mixed, weight_sum, bias_sum,
+    groups, rels, head_rows, weights, biases, flat, left, right, left_mixed, right_mixed, near, own,
+    cotangent, state, grad_mixed, left_slope, right_slope, weight_sum, bias_sum,
     source, target, rel, tail, left_buf, right_buf, left_mixed_buf, right_mixed_buf, table_buf, own_buf,
-    cotangent_buf, window, grad_mixed_buf, state_buf, wide_sum, sems, *sums,
+    cotangent_buf, window, grad_mixed_buf, state_buf, left_slope_buf, right_slope_buf, wide_sum, sems, *sums,
 ):
     long = sums[0].shape[0]
     states = fetch(
@@ -375,13 +408,18 @@
         + [(right_mixed, right_mixed_buf), (near, sums[0])],
         sems.at[pl.ds(5, 5)],
     )
-    lists = fetch_lists(flat, (source, target, rel, tail), tables, 1, table_buf, sems)
+    lists = fetch_lists(flat, (source, target, rel, tail), sems)
+    make_table(rels, 1, table_buf)
     clear(sums[1:])
-    first = split(weights[0])
+    first = split(block_weight(weights[0]))
+    first_bias = block_bias(biases[0:1, :])
     wait(states[:2])
-    advance(left_buf, left_mixed_buf, window, 0, first, biases[0])
+    advance(left_buf, left_mixed_buf, window, 0, first, first_bias, left_slope_buf)
     wait(states[2:])
-    advance(right_buf, right_mixed_buf, window, long, first, biases[0])
+    advance(right_buf, right_mixed_buf, window, long, first, first_bias, right_slope_buf)
+    stores = fetch(
+        [(left_slope_buf, left_slope), (right_slope_buf, right_slope)], sems.at[pl.ds(14, 2)]
+    )
     wait(lists)
     extra = fetch([(own, own_buf), (cotangent, cotangent_buf)], sems.at[pl.ds(10, 2)])
     add_boundary(groups, tail, head_rows, sums[0], long)
@@ -389,9 +427,10 @@
     wait(extra)
     spread(own_buf, window, 0)
     spread(cotangent_buf, window, long)
-    wide = split_weight(weights[1])
-    wide_back = split_weight(weights[1].T)
-    bias = biases[1]
+    weight = block_weight(weights[1])
+    wide = split_weight(weight)
+    wide_back = split_weight(weight.T)
+    bias = block_bias(biases[1:2, :])
     wide_sum[...] = jnp.zeros_like(wide_sum)
     bias_sum[...] = jnp.zeros_like(bias_sum)
 
@@ -402,14 +441,14 @@
         values = times(mix, wide) + bias
         sigma = jax.nn.sigmoid(values)
         window[rows, :] += values * sigma
-        grad = window[pl.ds(long + at, DENSE), :] * (sigma * (1.0 + values * (1.0 - sigma)))
+        grad = window[pl.ds(long + at, DENSE), :] * slope_from(values, sigma)
         grad_mixed_buf[rows, :] = times(grad, wide_back).astype(jnp.bfloat16)
         wide_sum[...] += outer(mix, grad)
         bias_sum[...] += jnp.sum(grad, axis=0, keepdims=True)
         return carry
 
     lax.fori_loop(0, long // DENSE, step, 0)
-    stores = fetch([(grad_mixed_buf, grad_mixed)], sems.at[pl.ds(12, 1)])
+    stores += fetch([(grad_mixed_buf, grad_mixed)], sems.at[pl.ds(12, 1)])
     size = CHUNK // groups
 
     def store(i, carry):
@@ -440,43 +479,60 @@
     return value
 
 
+def prepare_kernel(
+    weights, biases, cotangent, own, mirror, own_slope, mirror_slope, weight_sum, bias_sum, window, wide_sum
+):
+    spread(cotangent, window, 0)
+    wide = split(block_weight(weights[0]))
+    bias = block_bias(biases[0:1, :])
+    wide_sum[...] = jnp.zeros_like(wide_sum)
+    bias_sum[...] = jnp.zeros_like(bias_sum)
+
+    def step(i, carry):
+        rows = pl.ds(pl.multiple_of(i * DENSE, DENSE), DENSE)
+        values = update_of(mirror[rows, :], wide, bias)
+        mirror_slope[rows, :] = slope_from(values, jax.nn.sigmoid(values))
+        mixed = own[rows, :]
+        values = update_of(mixed, wide, bias)
+        slope = slope_from(values, jax.nn.sigmoid(values))
+        own_slope[rows, :] = slope
+        grad = window[rows, :] * slope
+        wide_sum[...] += outer_rounded(mixed, grad)
+        bias_sum[...] += jnp.sum(grad, axis=0, keepdims=True)
+        return carry
+
+    lax.fori_loop(0, window.shape[0] // DENSE, step, 0)
+    weight_sum[...] = wide_sum[:, :LANES] + wide_sum[:, LANES:]
+
+
 def adjoint_kernel(
-    groups, weights, biases, weight_one, bias_one, flat, grad_mixed, tables, cotangent, own, mirror, left,
-    right, out,
-    source, target, rel, tail, grad_mixed_buf, table_buf, cotangent_buf, own_buf, mirror_buf, left_buf,
-    right_buf, window, wide_sum, bias_sum, sems, *sums,
+    groups, rels, weight_zero, bias_zero, weight_one, bias_one, flat, grad_mixed, *refs
 ):
+    parts, refs = refs[:8], refs[8:]
+    out, source, target, rel, tail, grad_mixed_buf, table_buf = refs[:7]
+    bufs, refs = refs[7:15], refs[15:]
+    window, wide_sum, bias_sum, sems = refs[:4]
+    sums = refs[4:]
     long = window.shape[0]
-    lists = fetch_lists(flat, (source, target, rel, tail), tables, 1, table_buf, sems)
+    lists = fetch_lists(flat, (source, target, rel, tail), sems)
     loads = fetch([(grad_mixed, grad_mixed_buf)], sems.at[pl.ds(5, 1)])
+    make_table(rels, 1, table_buf)
     clear(sums)
     wide_sum[...] = jnp.zeros_like(wide_sum)
-    bias_sum[...] = jnp.zeros_like(bias_sum)
-    wide = split(weights[0])
-    bias = biases[0]
+    bias_sum[...] = bias_zero[...]
     wait(loads)
     spread(grad_mixed_buf, window, 0)
     wait(lists)
-    late = fetch(
-        [(left, left_buf), (right, right_buf), (mirror, mirror_buf), (own, own_buf)]
-        + [(cotangent, cotangent_buf)],
-        sems.at[pl.ds(6, 5)],
-    )
-
-    def add_products(mixed_buf, first, extra, again):
+    late = fetch(list(zip(parts, bufs)), sems.at[pl.ds(6, 8)])
+
+    def add_products(mixed_buf, slope_buf, first, again):
         def step(i, carry):
             at = pl.multiple_of(i * DENSE, DENSE)
-            terms = total_of(sums, first + at, DENSE)
-            if extra is not None:
-                terms = terms + extra[pl.ds(at, DENSE), :]
+            grad = total_of(sums, first + at, DENSE) * slope_buf[pl.ds(at, DENSE), :]
             if again:
                 for ref in sums:
                     ref[pl.ds(first + at, DENSE), :] = jnp.zeros((DENSE, LANES), jnp.float32)
-            mixed = mixed_buf[pl.ds(at, DENSE), :]
-            grad = terms * silu_slope(update_of(mixed, wide, bias))
-            wide_sum[...] += lax.dot_general(
-                mixed, split(grad), (((0,), (0,)), ((), ())), preferred_element_type=jnp.float32
-            )
+            wide_sum[...] += outer_rounded(mixed_buf[pl.ds(at, DENSE), :], grad)
             bias_sum[...] += jnp.sum(grad, axis=0, keepdims=True)
             return carry
 
@@ -484,14 +540,13 @@
 
     walk(groups, tail[1], tail[3], target, source, rel, window, table_buf, sums)
     wait(late)
-    add_products(left_buf, 0, None, True)
-    add_products(right_buf, long, None, True)
+    add_products(bufs[0], bufs[1], 0, True)
+    add_products(bufs[2], bufs[3], long, True)
     walk(groups, 0, tail[1], target, source, rel, window, table_buf, sums)
-    add_products(mirror_buf, long, None, False)
-    spread(cotangent_buf, window, 0)
-    add_products(own_buf, 0, window, False)
+    add_products(bufs[4], bufs[5], 0, False)
+    add_products(bufs[6], bufs[7], long, False)
     out[...] = jnp.zeros_like(out)
-    out[0:DIM, 0:DIM] = folded(wide_sum[:, :LANES] + wide_sum[:, LANES:])
+    out[0:DIM, 0:DIM] = folded(wide_sum[:, :LANES] + wide_sum[:, LANES:] + weight_zero[...])
     out[DIM : 2 * DIM, 0:DIM] = folded(weight_one[...])
     out[2 * DIM : 2 * DIM + 1, 0:DIM] = folded_row(bias_sum[...])
     out[2 * DIM + 1 : 2 * DIM + 2, 0:DIM] = folded_row(bias_one[...])
@@ -586,12 +641,9 @@
         jnp.tile(query_vec, (1, repeat)),
         0.0,
     )
-    tables = jnp.tile(jnp.pad(rel_vectors, ((0, 0), (0, -rel_count % 8 or 8), (0, 0))), (1, 1, repeat))
-    same = lane_group[:, None] == lane_group[None, :]
-    weights = jnp.where(same[None], jnp.tile(mix_weight, (1, repeat, repeat)), 0.0)
-    biases = jnp.tile(mix_bias, (1, repeat))[:, None, :]
+    rels = rel_vectors.transpose(0, 2, 1)
     list_bufs = [pltpu.SMEM((room,), jnp.int32)] * 3 + [pltpu.SMEM((tail_room,), jnp.int32)]
-    table_buf = pltpu.VMEM(tables.shape[1:], jnp.float32)
+    table_buf = pltpu.VMEM(((rel_count // LANES + 1) * LANES, LANES), jnp.float32)
 
     def sems(count):
         return pltpu.SemaphoreType.DMA((count,))
@@ -606,16 +658,16 @@
     mirror, left, right = halo(state_zero)
     near = run(
         functools.partial(near_zero_kernel, groups),
-        [flat, state_zero, mirror, tables],
-        [ANY] * 4,
+        [rels, flat, state_zero, mirror],
+        [VMEM] + [ANY] * 3,
         wide_f32,
         ANY,
         [*list_bufs, block_buf, block_buf, table_buf, pair, sems(11), *sums],
     )
     state_one, mixed = run(
         functools.partial(first_kernel, groups),
-        [head_rows, weights, biases, flat, left, right, near, tables, state_zero],
-        [VMEM] * 3 + [ANY] * 6,
+        [rels, head_rows, mix_weight, mix_bias, flat, left, right, near, state_zero],
+        [VMEM] * 4 + [ANY] * 5,
         [wide_bf16, wide_bf16],
         [ANY] * 2,
         [*list_bufs, block_buf, block_buf, table_buf, block_buf, pair, bf16_buf, bf16_buf, sems(17), *sums],
@@ -623,21 +675,31 @@
     mirror_mixed, left_mixed, right_mixed = halo(mixed)
     near = run(
         functools.partial(near_one_kernel, groups),
-        [weights, biases, flat, state_one, mirror, mirror_mixed, tables],
-        [VMEM] * 2 + [ANY] * 5,
+        [rels, mix_weight, mix_bias, flat, state_one, mirror, mirror_mixed],
+        [VMEM] * 3 + [ANY] * 4,
         wide_f32,
         ANY,
         [*list_bufs, bf16_buf, block_buf, bf16_buf, table_buf, pair, sems(12), *sums],
     )
-    state_two, grad_mixed, weight_one, bias_one = run(
+    own_slope, mirror_slope, weight_zero, bias_zero = run(
+        prepare_kernel,
+        [mix_weight, mix_bias, grad_out, mixed, mirror_mixed],
+        [VMEM] * 5,
+        [wide_f32, wide_f32, square, line],
+        [VMEM] * 4,
+        [f32_buf, pltpu.VMEM((LANES, 2 * LANES), jnp.float32)],
+    )
+    state_two, grad_mixed, left_slope, right_slope, weight_one, bias_one = run(
         functools.partial(second_kernel, groups),
-        [head_rows, weights, biases, flat, left, right, left_mixed, right_mixed, near, tables, state_one]
+        [rels, head_rows, mix_weight, mix_bias, flat, left, right, left_mixed, right_mixed, near, state_one]
         + [grad_out],
-        [VMEM] * 3 + [ANY] * 9,
-        [jax.ShapeDtypeStruct(entity_state.shape, jnp.bfloat16), wide_bf16, square, line],
-        [ANY] * 2 + [VMEM] * 2,
+        [VMEM] * 4 + [ANY] * 8,
+        [jax.ShapeDtypeStruct(entity_state.shape, jnp.bfloat16), wide_bf16, wide_f32, wide_f32]
+        + [square, line],
+        [ANY] * 4 + [VMEM] * 2,
         [*list_bufs, block_buf, block_buf, bf16_buf, bf16_buf, table_buf, bf16_buf, block_buf, pair]
-        + [bf16_buf, block_buf, pltpu.VMEM((2 * LANES, 2 * LANES), jnp.float32), sems(14), *sums],
+        + [bf16_buf, block_buf, f32_buf, f32_buf, pltpu.VMEM((2 * LANES, 2 * LANES), jnp.float32)]
+        + [sems(16), *sums],
     )
     final_state = run(
         copy_kernel, [send(state_two, seats.give_back())], [ANY],
@@ -645,13 +707,13 @@
     )
     grads = run(
         functools.partial(adjoint_kernel, groups),
-        [weights, biases, weight_one, bias_one, flat, grad_mixed, tables, grad_out, mixed, mirror_mixed]
-        + [left_mixed, right_mixed],
-        [VMEM] * 4 + [ANY] * 8,
+        [rels, weight_zero, bias_zero, weight_one, bias_one, flat, grad_mixed, left_mixed, left_slope]
+        + [right_mixed, right_slope, mixed, own_slope, mirror_mixed, mirror_slope],
+        [VMEM] * 5 + [ANY] * 10,
         jax.ShapeDtypeStruct((2 * DIM + 8, LANES), jnp.float32),
         VMEM,
-        [*list_bufs, bf16_buf, table_buf, block_buf, bf16_buf, bf16_buf, bf16_buf, bf16_buf, f32_buf]
-        + [pltpu.VMEM((LANES, 2 * LANES), jnp.float32), pltpu.VMEM((1, LANES), jnp.float32), sems(11)]
+        [*list_bufs, bf16_buf, table_buf, *([bf16_buf, f32_buf] * 4), f32_buf]
+        + [pltpu.VMEM((LANES, 2 * LANES), jnp.float32), pltpu.VMEM((1, LANES), jnp.float32), sems(14)]
         + pair_sums,
     )
     devices = seats.nodes * seats.queries

time: 209 us -> 223 us (1.067)
  waiting for transfers between devices: 48.7 us -> 73.4 us
  local copies, waits for them, and re-layouts: 15 us -> 7.31 us
  Pallas kernels: 116 us -> 112 us
    ppermute x15, waiting for transfers between devices: 48.7 us -> 73.4 us  [send(): return lax.ppermute(block, AXES, route)]
    another operation x6 -> x0, local copies, waits for them, and re-layouts: 7.63 us -> none  [the longest x2 3.39 us: body(): jnp.tile(jnp.pad(rel_vectors, ((0, 0), (0, -rel_count % 8 or 8), (0, 0)))...]
    pallas_call x6 -> x7, Pallas kernels: 98.4 us -> 94.3 us  [run(): pl.pallas_call(fn, out_shape=outs, in_specs=specs, out_specs=out_specs, s...]
  transfers between devices with their start and end apart: 15 -> 15, of which waited for: 9 -> 9; matrix products, arithmetic and copies ran while one was open for 7% -> 2% of each run, Pallas kernels for 38% -> 35%
where the time goes in v2:
time: 223 us; the launch traced here: 219 us
  Pallas kernels  112 us (50%)
  waiting for transfers between devices  73.4 us (33%)
  starting transfers between devices  21 us (9%)
  local copies, waits for them, and re-layouts  7.31 us (3%)
  other arithmetic  3.68 us (2%)
    pallas_call x7, Pallas kernels, run(): pl.pallas_call(fn, out_shape=outs, in_specs=specs, out_specs=out_specs, s...  94.3 us
    ppermute x15, waiting for transfers between devices, send(): return lax.ppermute(block, AXES, route)  73.4 us
    ppermute x15, starting transfers between devices, send(): return lax.ppermute(block, AXES, route)  21 us
    pallas_call x1, Pallas kernels, edge_lists(): pl.pallas_call(functools.partial(bucket_kernel, tile_count=tile_count, ro...  17.9 us
    unnamed x18, local copies, waits for them, and re-layouts  5.96 us
  transfers between devices with their start and end apart: 15, of which 9 were waited for; matrix products, arithmetic and copies ran while one was open for 2% of the time, Pallas kernels for 35%

profile of v2, /device:TPU:10, one launch (start us, length us, event | category | flops | bytes accessed | tf_op | source)
XLA Modules:
  0.0 218.7 jit_solution(14601225766687085775)
XLA Ops:
  0.6 2.6 %collective-permute-start.1 = (bf16[1024,512]{1,0:T(8,128)(2,1)}, bf16[1024,512]{1,0:T(8,128)(2,1)S(1)}, u32[]{:S(2)}, u32[]{:S(2)}) collective-permute-start(bf16[1024,512]{1,0:T(8,128)(2,1)} %param.9), channel_id=1, source_target_pairs={{0,0},{1,16},{2,2},{3,18},{4,4},{5,20},{6,6},{7,22},{8,12},{9,28},... | collective-permute-start | bytes 3145736 | tf_op jit(solution)/shard_map/ppermute | solution.py:604
  3.2 17.9 %bucket.1 = (s32[9216]{0:T(1024)}, s32[4]{0:T(128)}) custom-call(s32[3,16,512]{2,1,0:T(8,128)} %bitcast.9), custom_call_target="tpu_custom_call" | custom-call | tf_op jit(solution)/shard_map/bucket/pallas_call | solution.py:566
  23.3 5.6 %collective-permute-done.1.own = bf16[1024,512]{1,0:T(8,128)(2,1)S(1)} collective-permute-done((bf16[1024,512]{1,0:T(8,128)(2,1)}, bf16[1024,512]{1,0:T(8,128)(2,1)S(1)}, u32[]{:S(2)}, u32[]{:S(2)}) %collective-permute-start.1) | collective-permute-done | bytes 1048608 | tf_op jit(solution)/shard_map/ppermute | solution.py:604
  31.0 2.2 collective-permute-start
  33.2 23.1 %collective-permute-done.flat = s32[28672]{0:T(1024)S(1)} collective-permute-done((s32[28672]{0:T(1024)S(1)}, s32[28672]{0:T(1024)S(1)}, u32[]{:S(2)}, u32[]{:S(2)}) %collective-permute-start) | collective-permute-done | bytes 114720 | tf_op jit(solution)/shard_map/ppermute | solution.py:604
  58.3 12.9 %shard_map.112.near = f32[4096,128]{1,0:T(8,128)} custom-call(f32[2,32,822]{2,1,0:T(8,128)} %bitcast.4, s32[28672]{0:T(1024)} %copy-done.7, bf16[1024,512]{1,0:T(8,128)(2,1)} %copy-done.2, bf16[1024,512]{1,0:T(8,128)(2,1)} %copy-done.3), custom_call_target="tpu_custom_call" | custom-call | tf_op jit(solution)/shard_map/pallas_call | solution.py:607
  72.2 13.7 %shard_map.113 = (bf16[4096,128]{1,0:T(8,128)(2,1)}, bf16[4096,128]{1,0:T(8,128)(2,1)}) custom-call(f32[2,32,822]{2,1,0:T(8,128)} %bitcast.5, f32[16,128]{1,0:T(8,128)} %compare_select_fusion.head_rows, f32[2,32,32]{2,1,0:T(8,128)} %weights.7, f32[2,32]{1,0:T(2,128)} %biases.7, s32[28672]{0:T(1024)} %copy-done.7, ...), custom_call_target="tpu_custom_call" | custom-call | tf_op jit(solution)/shard_map/pallas_call | solution.py:607
  85.9 3.2 %collective-permute-start.7 = (bf16[4096,128]{1,0:T(8,128)(2,1)}, bf16[4096,128]{1,0:T(8,128)(2,1)S(1)}, u32[]{:S(2)}, u32[]{:S(2)}) collective-permute-start(bf16[4096,128]{1,0:T(8,128)(2,1)} %get-tuple-element.19.own.refs_4_), channel_id=1, source_target_pairs={{0,1},{16,17},{2,3},{18,19},{4,5},{20,21},{6,7},{22,23},{12,13},{2... | collective-permute-start | bytes 3145736 | tf_op jit(solution)/shard_map/ppermute | solution.py:604
  89.1 1.9 collective-permute-start.8
  91.0 3.6 %collective-permute-start.6 = (bf16[4096,128]{1,0:T(8,128)(2,1)}, bf16[4096,128]{1,0:T(8,128)(2,1)S(1)}, u32[]{:S(2)}, u32[]{:S(2)}) collective-permute-start(bf16[4096,128]{1,0:T(8,128)(2,1)} %get-tuple-element.19.own.refs_4_), channel_id=1, source_target_pairs={{4,0},{20,16},{6,2},{22,18},{12,4},{28,20},{14,6},{30,22},{8,12},{... | collective-permute-start | bytes 3145736 | tf_op jit(solution)/shard_map/ppermute | solution.py:604
  95.6 13.9 %shard_map.114.near = f32[4096,128]{1,0:T(8,128)} custom-call(f32[2,32,822]{2,1,0:T(8,128)} %bitcast.6, f32[2,32,32]{2,1,0:T(8,128)} %weights.7, f32[2,32]{1,0:T(2,128)} %biases.7, s32[28672]{0:T(1024)} %copy-done.7, bf16[4096,128]{1,0:T(8,128)(2,1)} %get-tuple-element.20.own, bf16[1024,512]{1,0:T(8,128)(2,1)} %copy-done.3, bf16[4096,128]{1,0:T(8,128)(2,1)} %copy-done.1), custom_call_target="tpu_custom_call" | custom-call | tf_op jit(solution)/shard_map/pallas_call | solution.py:607
  109.6 18.3 %collective-permute-done.8.cotangent = bf16[1024,512]{1,0:T(8,128)(2,1)} collective-permute-done((bf16[1024,512]{1,0:T(8,128)(2,1)}, bf16[1024,512]{1,0:T(8,128)(2,1)}, u32[]{:S(2)}, u32[]{:S(2)}) %collective-permute-start.8) | collective-permute-done | bytes 1048608 | tf_op jit(solution)/shard_map/ppermute | solution.py:604
  127.9 11.8 %collective-permute-done.6.right_mixed.refs_2_ = bf16[4096,128]{1,0:T(8,128)(2,1)S(1)} collective-permute-done((bf16[4096,128]{1,0:T(8,128)(2,1)}, bf16[4096,128]{1,0:T(8,128)(2,1)S(1)}, u32[]{:S(2)}, u32[]{:S(2)}) %collective-permute-start.6) | collective-permute-done | bytes 1048608 | tf_op jit(solution)/shard_map/ppermute | solution.py:604
  141.7 19.1 %shard_map.115 = (bf16[1024,512]{1,0:T(8,128)(2,1)}, bf16[4096,128]{1,0:T(8,128)(2,1)}, f32[4096,128]{1,0:T(8,128)}, f32[4096,128]{1,0:T(8,128)}, f32[128,128]{1,0:T(8,128)}, /*index=5*/f32[1,128]{1,0:T(1,128)}) custom-call(f32[2,32,822]{2,1,0:T(8,128)} %bitcast.7, f32[16,128]{1,0:T(8,128)} %compare_select_fusion.head_rows, f32[2,32,32]{2,1,0:T(8,128)} %weights.7, ...), custom_call_target="tpu_custom_call" | custom-call | tf_op jit(solution)/shard_map/pallas_call | solution.py:607
  160.8 1.9 collective-permute-start.9
  162.8 6.8 %shard_map.117 = (f32[4096,128]{1,0:T(8,128)}, f32[4096,128]{1,0:T(8,128)}, f32[128,128]{1,0:T(8,128)}, f32[1,128]{1,0:T(1,128)}) custom-call(f32[2,32,32]{2,1,0:T(8,128)} %weights.7, f32[2,32]{1,0:T(2,128)} %biases.7, bf16[1024,512]{1,0:T(8,128)(2,1)} %collective-permute-done.8.cotangent, bf16[4096,128]{1,0:T(8,128)(2,1)} %get-tuple-element.19.own.refs_4_, ...), custom_call_target="tpu_custom_call" | custom-call | tf_op jit(solution)/shard_map/pallas_call | solution.py:607
  169.6 25.7 %shard_map.118 = f32[72,128]{1,0:T(8,128)} custom-call(f32[2,32,822]{2,1,0:T(8,128)} %bitcast.8, f32[128,128]{1,0:T(8,128)} %get-tuple-element.22.weight_zero, f32[1,128]{1,0:T(1,128)} %get-tuple-element.23.bias_zero, f32[128,128]{1,0:T(8,128)} %get-tuple-element.24.weight_one, f32[1,128]{1,0:T(1,128)} %get-tuple-element.25.bias_one, s32[28672]{0:T(1024)} %copy-done.7, ...), custom_call_target="tpu_custom_call" | custom-call | tf_op jit(solution)/shard_map/pallas_call | solution.py:607
  197.5 1.5 collective-permute-start.11
  199.1 2.4 %collective-permute-done.11 = f32[72,128]{1,0:T(8,128)S(1)} collective-permute-done((f32[72,128]{1,0:T(8,128)S(1)}, f32[72,128]{1,0:T(8,128)S(1)}, u32[]{:S(2)}, u32[]{:S(2)}) %collective-permute-start.11) | collective-permute-done | bytes 36896 | tf_op jit(solution)/shard_map/ppermute | solution.py:604
  201.5 2.0 collective-permute-start.12
  203.5 1.9 collective-permute-done.12
  205.5 3.9 %collective-permute-done.13 = f32[72,128]{1,0:T(8,128)S(1)} collective-permute-done((f32[72,128]{1,0:T(8,128)S(1)}, f32[72,128]{1,0:T(8,128)S(1)}, u32[]{:S(2)}, u32[]{:S(2)}) %collective-permute-start.13) | collective-permute-done | bytes 36896 | tf_op jit(solution)/shard_map/ppermute | solution.py:604
  209.4 4.8 %collective-permute-done.14 = f32[72,128]{1,0:T(8,128)S(1)} collective-permute-done((f32[72,128]{1,0:T(8,128)S(1)}, f32[72,128]{1,0:T(8,128)S(1)}, u32[]{:S(2)}, u32[]{:S(2)}) %collective-permute-start.14) | collective-permute-done | bytes 36896 | tf_op jit(solution)/shard_map/ppermute | solution.py:604
  216.5 2.2 %shard_map.116 = bf16[1024,512]{1,0:T(8,128)(2,1)} custom-call(bf16[1024,512]{1,0:T(8,128)(2,1)} %copy-done.8), custom_call_target="tpu_custom_call" | custom-call | tf_op jit(solution)/shard_map/pallas_call | solution.py:607
  (50 shorter events, 14.7 us)
Async XLA Ops:
  0.6 55.7 %copy-start = (f32[822,32]{0,1:T(8,128)S(1)}, f32[822,32]{0,1:T(8,128)}, u32[]{:S(2)}) copy-start(f32[822,32]{0,1:T(8,128)} %param.13) | copy-start | bytes 315652
  0.6 28.3 %collective-permute-start.1 = (bf16[1024,512]{1,0:T(8,128)(2,1)}, bf16[1024,512]{1,0:T(8,128)(2,1)S(1)}, u32[]{:S(2)}, u32[]{:S(2)}) collective-permute-start(bf16[1024,512]{1,0:T(8,128)(2,1)} %param.9), channel_id=1, source_target_pairs={{0,0},{1,16},{2,2},{3,18},{4,4},{5,20},{6,6},{7,22},{8,12},{9,28},... | collective-permute-start | bytes 3145736 | tf_op jit(solution)/shard_map/ppermute | solution.py:604
  28.9 28.4 %copy-start.2 = (bf16[1024,512]{1,0:T(8,128)(2,1)}, bf16[1024,512]{1,0:T(8,128)(2,1)S(1)}, u32[]{:S(2)}) copy-start(bf16[1024,512]{1,0:T(8,128)(2,1)S(1)} %collective-permute-done.1.own) | copy-start | bytes 3145732
  28.9 28.4 %collective-permute-start.4 = (bf16[1024,512]{1,0:T(8,128)(2,1)S(1)}, bf16[1024,512]{1,0:T(8,128)(2,1)S(1)}, u32[]{:S(2)}, u32[]{:S(2)}) collective-permute-start(bf16[1024,512]{1,0:T(8,128)(2,1)S(1)} %collective-permute-done.1.own), channel_id=1, source_target_pairs={{0,1},{16,17},{2,3},{18,19},{4,5},{20,21},{6,7},{22,23},{12,13},{2... | collective-permute-start | bytes 3145736 | tf_op jit(solution)/shard_map/ppermute | solution.py:604
  28.9 42.3 %collective-permute-start.3 = (bf16[1024,512]{1,0:T(8,128)(2,1)S(1)}, bf16[1024,512]{1,0:T(8,128)(2,1)S(1)}, u32[]{:S(2)}, u32[]{:S(2)}) collective-permute-start(bf16[1024,512]{1,0:T(8,128)(2,1)S(1)} %collective-permute-done.1.own), channel_id=1, source_target_pairs={{4,0},{20,16},{6,2},{22,18},{12,4},{28,20},{14,6},{30,22},{8,12},{... | collective-permute-start | bytes 3145736 | tf_op jit(solution)/shard_map/ppermute | solution.py:604
  29.8 41.5 %collective-permute-start.2 = (bf16[1024,512]{1,0:T(8,128)(2,1)S(1)}, bf16[1024,512]{1,0:T(8,128)(2,1)}, u32[]{:S(2)}, u32[]{:S(2)}) collective-permute-start(bf16[1024,512]{1,0:T(8,128)(2,1)S(1)} %collective-permute-done.1.own), channel_id=1, source_target_pairs={{9,0},{25,16},{11,2},{27,18},{0,4},{16,20},{2,6},{18,22},{4,12},{2... | collective-permute-start | bytes 3145736 | tf_op jit(solution)/shard_map/ppermute | solution.py:604
  31.0 25.3 %collective-permute-start = (s32[28672]{0:T(1024)S(1)}, s32[28672]{0:T(1024)S(1)}, u32[]{:S(2)}, u32[]{:S(2)}) collective-permute-start(s32[28672]{0:T(1024)S(1)} %pad_add_fusion), channel_id=1, source_target_pairs={{0,0},{1,16},{2,2},{3,18},{4,4},{5,20},{6,6},{7,22},{8,12},{9,28},... | collective-permute-start | bytes 344072 | tf_op jit(solution)/shard_map/ppermute | solution.py:604
  56.2 1.1 copy-start.7
  57.3 1.0 copy-start.3
  71.2 1.0 copy-start.6
  85.9 8.7 %collective-permute-start.7 = (bf16[4096,128]{1,0:T(8,128)(2,1)}, bf16[4096,128]{1,0:T(8,128)(2,1)S(1)}, u32[]{:S(2)}, u32[]{:S(2)}) collective-permute-start(bf16[4096,128]{1,0:T(8,128)(2,1)} %get-tuple-element.19.own.refs_4_), channel_id=1, source_target_pairs={{0,1},{16,17},{2,3},{18,19},{4,5},{20,21},{6,7},{22,23},{12,13},{2... | collective-permute-start | bytes 3145736 | tf_op jit(solution)/shard_map/ppermute | solution.py:604
  89.1 38.8 %collective-permute-start.8 = (bf16[1024,512]{1,0:T(8,128)(2,1)}, bf16[1024,512]{1,0:T(8,128)(2,1)}, u32[]{:S(2)}, u32[]{:S(2)}) collective-permute-start(bf16[1024,512]{1,0:T(8,128)(2,1)} %param.17), channel_id=1, source_target_pairs={{0,0},{1,16},{2,2},{3,18},{4,4},{5,20},{6,6},{7,22},{8,12},{9,28},... | collective-permute-start | bytes 3145736 | tf_op jit(solution)/shard_map/ppermute | solution.py:604
  91.0 48.7 %collective-permute-start.6 = (bf16[4096,128]{1,0:T(8,128)(2,1)}, bf16[4096,128]{1,0:T(8,128)(2,1)S(1)}, u32[]{:S(2)}, u32[]{:S(2)}) collective-permute-start(bf16[4096,128]{1,0:T(8,128)(2,1)} %get-tuple-element.19.own.refs_4_), channel_id=1, source_target_pairs={{4,0},{20,16},{6,2},{22,18},{12,4},{28,20},{14,6},{30,22},{8,12},{... | collective-permute-start | bytes 3145736 | tf_op jit(solution)/shard_map/ppermute | solution.py:604
  94.7 45.1 %collective-permute-start.5 = (bf16[4096,128]{1,0:T(8,128)(2,1)}, bf16[4096,128]{1,0:T(8,128)(2,1)S(1)}, u32[]{:S(2)}, u32[]{:S(2)}) collective-permute-start(bf16[4096,128]{1,0:T(8,128)(2,1)} %get-tuple-element.19.own.refs_4_), channel_id=1, source_target_pairs={{9,0},{25,16},{11,2},{27,18},{0,4},{16,20},{2,6},{18,22},{4,12},{2... | collective-permute-start | bytes 3145736 | tf_op jit(solution)/shard_map/ppermute | solution.py:604
  94.7 1.0 copy-start.1
  139.7 1.0 copy-start.4
  140.7 1.0 copy-start.5
  160.8 54.6 %collective-permute-start.9 = (bf16[1024,512]{1,0:T(8,128)(2,1)}, bf16[1024,512]{1,0:T(8,128)(2,1)S(1)}, u32[]{:S(2)}, u32[]{:S(2)}) collective-permute-start(bf16[1024,512]{1,0:T(8,128)(2,1)} %get-tuple-element.21), channel_id=1, source_target_pairs={{0,0},{16,1},{2,2},{18,3},{4,4},{20,5},{6,6},{22,7},{12,8},{28,9},... | collective-permute-start | bytes 3145736 | tf_op jit(solution)/shard_map/ppermute | solution.py:604
  195.3 1.5 collective-permute-start.10
  197.5 4.0 %collective-permute-start.11 = (f32[72,128]{1,0:T(8,128)S(1)}, f32[72,128]{1,0:T(8,128)S(1)}, u32[]{:S(2)}, u32[]{:S(2)}) collective-permute-start(f32[72,128]{1,0:T(8,128)S(1)} %add.33), channel_id=1, source_target_pairs={{0,2},{1,3},{2,0},{3,1},{4,6},{5,7},{6,4},{7,5},{8,10},{9,11},{10,... | collective-permute-start | bytes 110600 | tf_op jit(solution)/shard_map/ppermute | solution.py:604
  201.5 4.0 %collective-permute-start.12 = (f32[72,128]{1,0:T(8,128)S(1)}, f32[72,128]{1,0:T(8,128)S(1)}, u32[]{:S(2)}, u32[]{:S(2)}) collective-permute-start(f32[72,128]{1,0:T(8,128)S(1)} %add.34), channel_id=1, source_target_pairs={{0,4},{1,5},{2,6},{3,7},{4,0},{5,1},{6,2},{7,3},{8,12},{9,13},{10,... | collective-permute-start | bytes 110600 | tf_op jit(solution)/shard_map/ppermute | solution.py:604
  205.5 4.0 %collective-permute-start.13 = (f32[72,128]{1,0:T(8,128)S(1)}, f32[72,128]{1,0:T(8,128)S(1)}, u32[]{:S(2)}, u32[]{:S(2)}) collective-permute-start(f32[72,128]{1,0:T(8,128)S(1)} %add.35), channel_id=1, source_target_pairs={{0,8},{1,9},{2,10},{3,11},{4,12},{5,13},{6,14},{7,15},{8,0},{9,1},... | collective-permute-start | bytes 110600 | tf_op jit(solution)/shard_map/ppermute | solution.py:604
  209.4 4.9 %collective-permute-start.14 = (f32[72,128]{1,0:T(8,128)S(1)}, f32[72,128]{1,0:T(8,128)S(1)}, u32[]{:S(2)}, u32[]{:S(2)}) collective-permute-start(f32[72,128]{1,0:T(8,128)S(1)} %add.36), channel_id=1, source_target_pairs={{0,16},{1,17},{2,18},{3,19},{4,20},{5,21},{6,22},{7,23},{8,24},{9,... | collective-permute-start | bytes 110600 | tf_op jit(solution)/shard_map/ppermute | solution.py:604
  215.5 1.0 copy-start.8

commit v3 on v2

--- a/solution.py
+++ b/solution.py
@@ -19,7 +19,7 @@
 HIGHEST = lax.Precision.HIGHEST
 SMEM = pl.BlockSpec(memory_space=pltpu.SMEM)
 VMEM = pl.BlockSpec(memory_space=pltpu.VMEM)
-ANY = pl.BlockSpec(memory_space=pl.ANY)
+HBM = pl.BlockSpec(memory_space=pltpu.HBM)
 
 
 class Seats:
@@ -659,26 +659,26 @@
     near = run(
         functools.partial(near_zero_kernel, groups),
         [rels, flat, state_zero, mirror],
-        [VMEM] + [ANY] * 3,
+        [VMEM] + [HBM] * 3,
         wide_f32,
-        ANY,
+        HBM,
         [*list_bufs, block_buf, block_buf, table_buf, pair, sems(11), *sums],
     )
     state_one, mixed = run(
         functools.partial(first_kernel, groups),
         [rels, head_rows, mix_weight, mix_bias, flat, left, right, near, state_zero],
-        [VMEM] * 4 + [ANY] * 5,
+        [VMEM] * 4 + [HBM] * 5,
         [wide_bf16, wide_bf16],
-        [ANY] * 2,
+        [HBM] * 2,
         [*list_bufs, block_buf, block_buf, table_buf, block_buf, pair, bf16_buf, bf16_buf, sems(17), *sums],
     )
     mirror_mixed, left_mixed, right_mixed = halo(mixed)
     near = run(
         functools.partial(near_one_kernel, groups),
         [rels, mix_weight, mix_bias, flat, state_one, mirror, mirror_mixed],
-        [VMEM] * 3 + [ANY] * 4,
+        [VMEM] * 3 + [HBM] * 4,
         wide_f32,
-        ANY,
+        HBM,
         [*list_bufs, bf16_buf, block_buf, bf16_buf, table_buf, pair, sems(12), *sums],
     )
     own_slope, mirror_slope, weight_zero, bias_zero = run(
@@ -693,23 +693,23 @@
         functools.partial(second_kernel, groups),
         [rels, head_rows, mix_weight, mix_bias, flat, left, right, left_mixed, right_mixed, near, state_one]
         + [grad_out],
-        [VMEM] * 4 + [ANY] * 8,
+        [VMEM] * 4 + [HBM] * 8,
         [jax.ShapeDtypeStruct(entity_state.shape, jnp.bfloat16), wide_bf16, wide_f32, wide_f32]
         + [square, line],
-        [ANY] * 4 + [VMEM] * 2,
+        [HBM] * 4 + [VMEM] * 2,
         [*list_bufs, block_buf, block_buf, bf16_buf, bf16_buf, table_buf, bf16_buf, block_buf, pair]
         + [bf16_buf, block_buf, f32_buf, f32_buf, pltpu.VMEM((2 * LANES, 2 * LANES), jnp.float32)]
         + [sems(16), *sums],
     )
     final_state = run(
-        copy_kernel, [send(state_two, seats.give_back())], [ANY],
+        copy_kernel, [send(state_two, seats.give_back())], [HBM],
         jax.ShapeDtypeStruct(entity_state.shape, jnp.bfloat16), VMEM, [sems(1)],
     )
     grads = run(
         functools.partial(adjoint_kernel, groups),
         [rels, weight_zero, bias_zero, weight_one, bias_one, flat, grad_mixed, left_mixed, left_slope]
         + [right_mixed, right_slope, mixed, own_slope, mirror_mixed, mirror_slope],
-        [VMEM] * 5 + [ANY] * 10,
+        [VMEM] * 5 + [HBM] * 10,
         jax.ShapeDtypeStruct((2 * DIM + 8, LANES), jnp.float32),
         VMEM,
         [*list_bufs, bf16_buf, table_buf, *([bf16_buf, f32_buf] * 4), f32_buf]

time: 223 us -> 223 us (level)
  no operation moved by 1% of the time
where the time goes in v3:
time: 223 us; the launch traced here: 219 us
  Pallas kernels  112 us (50%)
  waiting for transfers between devices  73.4 us (33%)
  starting transfers between devices  21 us (9%)
  local copies, waits for them, and re-layouts  7.31 us (3%)
  other arithmetic  3.68 us (2%)
    pallas_call x7, Pallas kernels, run(): pl.pallas_call(fn, out_shape=outs, in_specs=specs, out_specs=out_specs, s...  94.3 us
    ppermute x15, waiting for transfers between devices, send(): return lax.ppermute(block, AXES, route)  73.4 us
    ppermute x15, starting transfers between devices, send(): return lax.ppermute(block, AXES, route)  21 us
    pallas_call x1, Pallas kernels, edge_lists(): pl.pallas_call(functools.partial(bucket_kernel, tile_count=tile_count, ro...  17.9 us
    unnamed x18, local copies, waits for them, and re-layouts  5.96 us
  transfers between devices with their start and end apart: 15, of which 9 were waited for; matrix products, arithmetic and copies ran while one was open for 2% of the time, Pallas kernels for 35%

profile of v3, /device:TPU:10, one launch (start us, length us, event | category | flops | bytes accessed | tf_op | source)
XLA Modules:
  0.0 218.7 jit_solution(14601225766687085775)
XLA Ops:
  0.6 2.6 %collective-permute-start.1 = (bf16[1024,512]{1,0:T(8,128)(2,1)}, bf16[1024,512]{1,0:T(8,128)(2,1)S(1)}, u32[]{:S(2)}, u32[]{:S(2)}) collective-permute-start(bf16[1024,512]{1,0:T(8,128)(2,1)} %param.9), channel_id=1, source_target_pairs={{0,0},{1,16},{2,2},{3,18},{4,4},{5,20},{6,6},{7,22},{8,12},{9,28},... | collective-permute-start | bytes 3145736 | tf_op jit(solution)/shard_map/ppermute | solution.py:604
  3.2 17.9 %bucket.1 = (s32[9216]{0:T(1024)}, s32[4]{0:T(128)}) custom-call(s32[3,16,512]{2,1,0:T(8,128)} %bitcast.9), custom_call_target="tpu_custom_call" | custom-call | tf_op jit(solution)/shard_map/bucket/pallas_call | solution.py:566
  23.3 5.6 %collective-permute-done.1.own = bf16[1024,512]{1,0:T(8,128)(2,1)S(1)} collective-permute-done((bf16[1024,512]{1,0:T(8,128)(2,1)}, bf16[1024,512]{1,0:T(8,128)(2,1)S(1)}, u32[]{:S(2)}, u32[]{:S(2)}) %collective-permute-start.1) | collective-permute-done | bytes 1048608 | tf_op jit(solution)/shard_map/ppermute | solution.py:604
  31.0 2.2 collective-permute-start
  33.2 23.1 %collective-permute-done.flat = s32[28672]{0:T(1024)S(1)} collective-permute-done((s32[28672]{0:T(1024)S(1)}, s32[28672]{0:T(1024)S(1)}, u32[]{:S(2)}, u32[]{:S(2)}) %collective-permute-start) | collective-permute-done | bytes 114720 | tf_op jit(solution)/shard_map/ppermute | solution.py:604
  58.3 12.9 %shard_map.112.near = f32[4096,128]{1,0:T(8,128)} custom-call(f32[2,32,822]{2,1,0:T(8,128)} %bitcast.4, s32[28672]{0:T(1024)} %copy-done.7, bf16[1024,512]{1,0:T(8,128)(2,1)} %copy-done.2, bf16[1024,512]{1,0:T(8,128)(2,1)} %copy-done.3), custom_call_target="tpu_custom_call" | custom-call | tf_op jit(solution)/shard_map/pallas_call | solution.py:607
  72.2 13.7 %shard_map.113 = (bf16[4096,128]{1,0:T(8,128)(2,1)}, bf16[4096,128]{1,0:T(8,128)(2,1)}) custom-call(f32[2,32,822]{2,1,0:T(8,128)} %bitcast.5, f32[16,128]{1,0:T(8,128)} %compare_select_fusion.head_rows, f32[2,32,32]{2,1,0:T(8,128)} %weights.7, f32[2,32]{1,0:T(2,128)} %biases.7, s32[28672]{0:T(1024)} %copy-done.7, ...), custom_call_target="tpu_custom_call" | custom-call | tf_op jit(solution)/shard_map/pallas_call | solution.py:607
  85.9 3.2 %collective-permute-start.7 = (bf16[4096,128]{1,0:T(8,128)(2,1)}, bf16[4096,128]{1,0:T(8,128)(2,1)S(1)}, u32[]{:S(2)}, u32[]{:S(2)}) collective-permute-start(bf16[4096,128]{1,0:T(8,128)(2,1)} %get-tuple-element.19.own.refs_4_), channel_id=1, source_target_pairs={{0,1},{16,17},{2,3},{18,19},{4,5},{20,21},{6,7},{22,23},{12,13},{2... | collective-permute-start | bytes 3145736 | tf_op jit(solution)/shard_map/ppermute | solution.py:604
  89.1 1.9 collective-permute-start.8
  91.0 3.6 %collective-permute-start.6 = (bf16[4096,128]{1,0:T(8,128)(2,1)}, bf16[4096,128]{1,0:T(8,128)(2,1)S(1)}, u32[]{:S(2)}, u32[]{:S(2)}) collective-permute-start(bf16[4096,128]{1,0:T(8,128)(2,1)} %get-tuple-element.19.own.refs_4_), channel_id=1, source_target_pairs={{4,0},{20,16},{6,2},{22,18},{12,4},{28,20},{14,6},{30,22},{8,12},{... | collective-permute-start | bytes 3145736 | tf_op jit(solution)/shard_map/ppermute | solution.py:604
  95.6 13.9 %shard_map.114.near = f32[4096,128]{1,0:T(8,128)} custom-call(f32[2,32,822]{2,1,0:T(8,128)} %bitcast.6, f32[2,32,32]{2,1,0:T(8,128)} %weights.7, f32[2,32]{1,0:T(2,128)} %biases.7, s32[28672]{0:T(1024)} %copy-done.7, bf16[4096,128]{1,0:T(8,128)(2,1)} %get-tuple-element.20.own, bf16[1024,512]{1,0:T(8,128)(2,1)} %copy-done.3, bf16[4096,128]{1,0:T(8,128)(2,1)} %copy-done.1), custom_call_target="tpu_custom_call" | custom-call | tf_op jit(solution)/shard_map/pallas_call | solution.py:607
  109.6 18.3 %collective-permute-done.8.cotangent = bf16[1024,512]{1,0:T(8,128)(2,1)} collective-permute-done((bf16[1024,512]{1,0:T(8,128)(2,1)}, bf16[1024,512]{1,0:T(8,128)(2,1)}, u32[]{:S(2)}, u32[]{:S(2)}) %collective-permute-start.8) | collective-permute-done | bytes 1048608 | tf_op jit(solution)/shard_map/ppermute | solution.py:604
  127.9 11.8 %collective-permute-done.6.right_mixed.refs_2_ = bf16[4096,128]{1,0:T(8,128)(2,1)S(1)} collective-permute-done((bf16[4096,128]{1,0:T(8,128)(2,1)}, bf16[4096,128]{1,0:T(8,128)(2,1)S(1)}, u32[]{:S(2)}, u32[]{:S(2)}) %collective-permute-start.6) | collective-permute-done | bytes 1048608 | tf_op jit(solution)/shard_map/ppermute | solution.py:604
  141.7 19.1 %shard_map.115 = (bf16[1024,512]{1,0:T(8,128)(2,1)}, bf16[4096,128]{1,0:T(8,128)(2,1)}, f32[4096,128]{1,0:T(8,128)}, f32[4096,128]{1,0:T(8,128)}, f32[128,128]{1,0:T(8,128)}, /*index=5*/f32[1,128]{1,0:T(1,128)}) custom-call(f32[2,32,822]{2,1,0:T(8,128)} %bitcast.7, f32[16,128]{1,0:T(8,128)} %compare_select_fusion.head_rows, f32[2,32,32]{2,1,0:T(8,128)} %weights.7, ...), custom_call_target="tpu_custom_call" | custom-call | tf_op jit(solution)/shard_map/pallas_call | solution.py:607
  160.8 1.9 collective-permute-start.9
  162.8 6.8 %shard_map.117 = (f32[4096,128]{1,0:T(8,128)}, f32[4096,128]{1,0:T(8,128)}, f32[128,128]{1,0:T(8,128)}, f32[1,128]{1,0:T(1,128)}) custom-call(f32[2,32,32]{2,1,0:T(8,128)} %weights.7, f32[2,32]{1,0:T(2,128)} %biases.7, bf16[1024,512]{1,0:T(8,128)(2,1)} %collective-permute-done.8.cotangent, bf16[4096,128]{1,0:T(8,128)(2,1)} %get-tuple-element.19.own.refs_4_, ...), custom_call_target="tpu_custom_call" | custom-call | tf_op jit(solution)/shard_map/pallas_call | solution.py:607
  169.6 25.7 %shard_map.118 = f32[72,128]{1,0:T(8,128)} custom-call(f32[2,32,822]{2,1,0:T(8,128)} %bitcast.8, f32[128,128]{1,0:T(8,128)} %get-tuple-element.22.weight_zero, f32[1,128]{1,0:T(1,128)} %get-tuple-element.23.bias_zero, f32[128,128]{1,0:T(8,128)} %get-tuple-element.24.weight_one, f32[1,128]{1,0:T(1,128)} %get-tuple-element.25.bias_one, s32[28672]{0:T(1024)} %copy-done.7, ...), custom_call_target="tpu_custom_call" | custom-call | tf_op jit(solution)/shard_map/pallas_call | solution.py:607
  197.5 1.5 collective-permute-start.11
  199.1 2.4 %collective-permute-done.11 = f32[72,128]{1,0:T(8,128)S(1)} collective-permute-done((f32[72,128]{1,0:T(8,128)S(1)}, f32[72,128]{1,0:T(8,128)S(1)}, u32[]{:S(2)}, u32[]{:S(2)}) %collective-permute-start.11) | collective-permute-done | bytes 36896 | tf_op jit(solution)/shard_map/ppermute | solution.py:604
  201.5 2.0 collective-permute-start.12
  203.5 1.9 collective-permute-done.12
  205.5 3.9 %collective-permute-done.13 = f32[72,128]{1,0:T(8,128)S(1)} collective-permute-done((f32[72,128]{1,0:T(8,128)S(1)}, f32[72,128]{1,0:T(8,128)S(1)}, u32[]{:S(2)}, u32[]{:S(2)}) %collective-permute-start.13) | collective-permute-done | bytes 36896 | tf_op jit(solution)/shard_map/ppermute | solution.py:604
  209.4 4.8 %collective-permute-done.14 = f32[72,128]{1,0:T(8,128)S(1)} collective-permute-done((f32[72,128]{1,0:T(8,128)S(1)}, f32[72,128]{1,0:T(8,128)S(1)}, u32[]{:S(2)}, u32[]{:S(2)}) %collective-permute-start.14) | collective-permute-done | bytes 36896 | tf_op jit(solution)/shard_map/ppermute | solution.py:604
  216.5 2.2 %shard_map.116 = bf16[1024,512]{1,0:T(8,128)(2,1)} custom-call(bf16[1024,512]{1,0:T(8,128)(2,1)} %copy-done.8), custom_call_target="tpu_custom_call" | custom-call | tf_op jit(solution)/shard_map/pallas_call | solution.py:607
  (50 shorter events, 14.7 us)
Async XLA Ops:
  0.6 55.7 %copy-start = (f32[822,32]{0,1:T(8,128)S(1)}, f32[822,32]{0,1:T(8,128)}, u32[]{:S(2)}) copy-start(f32[822,32]{0,1:T(8,128)} %param.13) | copy-start | bytes 315652
  0.6 28.3 %collective-permute-start.1 = (bf16[1024,512]{1,0:T(8,128)(2,1)}, bf16[1024,512]{1,0:T(8,128)(2,1)S(1)}, u32[]{:S(2)}, u32[]{:S(2)}) collective-permute-start(bf16[1024,512]{1,0:T(8,128)(2,1)} %param.9), channel_id=1, source_target_pairs={{0,0},{1,16},{2,2},{3,18},{4,4},{5,20},{6,6},{7,22},{8,12},{9,28},... | collective-permute-start | bytes 3145736 | tf_op jit(solution)/shard_map/ppermute | solution.py:604
  28.9 28.4 %copy-start.2 = (bf16[1024,512]{1,0:T(8,128)(2,1)}, bf16[1024,512]{1,0:T(8,128)(2,1)S(1)}, u32[]{:S(2)}) copy-start(bf16[1024,512]{1,0:T(8,128)(2,1)S(1)} %collective-permute-done.1.own) | copy-start | bytes 3145732
  28.9 28.4 %collective-permute-start.4 = (bf16[1024,512]{1,0:T(8,128)(2,1)S(1)}, bf16[1024,512]{1,0:T(8,128)(2,1)S(1)}, u32[]{:S(2)}, u32[]{:S(2)}) collective-permute-start(bf16[1024,512]{1,0:T(8,128)(2,1)S(1)} %collective-permute-done.1.own), channel_id=1, source_target_pairs={{0,1},{16,17},{2,3},{18,19},{4,5},{20,21},{6,7},{22,23},{12,13},{2... | collective-permute-start | bytes 3145736 | tf_op jit(solution)/shard_map/ppermute | solution.py:604
  28.9 42.3 %collective-permute-start.3 = (bf16[1024,512]{1,0:T(8,128)(2,1)S(1)}, bf16[1024,512]{1,0:T(8,128)(2,1)S(1)}, u32[]{:S(2)}, u32[]{:S(2)}) collective-permute-start(bf16[1024,512]{1,0:T(8,128)(2,1)S(1)} %collective-permute-done.1.own), channel_id=1, source_target_pairs={{4,0},{20,16},{6,2},{22,18},{12,4},{28,20},{14,6},{30,22},{8,12},{... | collective-permute-start | bytes 3145736 | tf_op jit(solution)/shard_map/ppermute | solution.py:604
  29.8 41.5 %collective-permute-start.2 = (bf16[1024,512]{1,0:T(8,128)(2,1)S(1)}, bf16[1024,512]{1,0:T(8,128)(2,1)}, u32[]{:S(2)}, u32[]{:S(2)}) collective-permute-start(bf16[1024,512]{1,0:T(8,128)(2,1)S(1)} %collective-permute-done.1.own), channel_id=1, source_target_pairs={{9,0},{25,16},{11,2},{27,18},{0,4},{16,20},{2,6},{18,22},{4,12},{2... | collective-permute-start | bytes 3145736 | tf_op jit(solution)/shard_map/ppermute | solution.py:604
  31.0 25.3 %collective-permute-start = (s32[28672]{0:T(1024)S(1)}, s32[28672]{0:T(1024)S(1)}, u32[]{:S(2)}, u32[]{:S(2)}) collective-permute-start(s32[28672]{0:T(1024)S(1)} %pad_add_fusion), channel_id=1, source_target_pairs={{0,0},{1,16},{2,2},{3,18},{4,4},{5,20},{6,6},{7,22},{8,12},{9,28},... | collective-permute-start | bytes 344072 | tf_op jit(solution)/shard_map/ppermute | solution.py:604
  56.2 1.1 copy-start.7
  57.3 1.0 copy-start.3
  71.2 1.0 copy-start.6
  85.9 8.7 %collective-permute-start.7 = (bf16[4096,128]{1,0:T(8,128)(2,1)}, bf16[4096,128]{1,0:T(8,128)(2,1)S(1)}, u32[]{:S(2)}, u32[]{:S(2)}) collective-permute-start(bf16[4096,128]{1,0:T(8,128)(2,1)} %get-tuple-element.19.own.refs_4_), channel_id=1, source_target_pairs={{0,1},{16,17},{2,3},{18,19},{4,5},{20,21},{6,7},{22,23},{12,13},{2... | collective-permute-start | bytes 3145736 | tf_op jit(solution)/shard_map/ppermute | solution.py:604
  89.1 38.8 %collective-permute-start.8 = (bf16[1024,512]{1,0:T(8,128)(2,1)}, bf16[1024,512]{1,0:T(8,128)(2,1)}, u32[]{:S(2)}, u32[]{:S(2)}) collective-permute-start(bf16[1024,512]{1,0:T(8,128)(2,1)} %param.17), channel_id=1, source_target_pairs={{0,0},{1,16},{2,2},{3,18},{4,4},{5,20},{6,6},{7,22},{8,12},{9,28},... | collective-permute-start | bytes 3145736 | tf_op jit(solution)/shard_map/ppermute | solution.py:604
  91.0 48.7 %collective-permute-start.6 = (bf16[4096,128]{1,0:T(8,128)(2,1)}, bf16[4096,128]{1,0:T(8,128)(2,1)S(1)}, u32[]{:S(2)}, u32[]{:S(2)}) collective-permute-start(bf16[4096,128]{1,0:T(8,128)(2,1)} %get-tuple-element.19.own.refs_4_), channel_id=1, source_target_pairs={{4,0},{20,16},{6,2},{22,18},{12,4},{28,20},{14,6},{30,22},{8,12},{... | collective-permute-start | bytes 3145736 | tf_op jit(solution)/shard_map/ppermute | solution.py:604
  94.7 45.1 %collective-permute-start.5 = (bf16[4096,128]{1,0:T(8,128)(2,1)}, bf16[4096,128]{1,0:T(8,128)(2,1)S(1)}, u32[]{:S(2)}, u32[]{:S(2)}) collective-permute-start(bf16[4096,128]{1,0:T(8,128)(2,1)} %get-tuple-element.19.own.refs_4_), channel_id=1, source_target_pairs={{9,0},{25,16},{11,2},{27,18},{0,4},{16,20},{2,6},{18,22},{4,12},{2... | collective-permute-start | bytes 3145736 | tf_op jit(solution)/shard_map/ppermute | solution.py:604
  94.7 1.0 copy-start.1
  139.7 1.0 copy-start.4
  140.7 1.0 copy-start.5
  160.8 54.6 %collective-permute-start.9 = (bf16[1024,512]{1,0:T(8,128)(2,1)}, bf16[1024,512]{1,0:T(8,128)(2,1)S(1)}, u32[]{:S(2)}, u32[]{:S(2)}) collective-permute-start(bf16[1024,512]{1,0:T(8,128)(2,1)} %get-tuple-element.21), channel_id=1, source_target_pairs={{0,0},{16,1},{2,2},{18,3},{4,4},{20,5},{6,6},{22,7},{12,8},{28,9},... | collective-permute-start | bytes 3145736 | tf_op jit(solution)/shard_map/ppermute | solution.py:604
  195.3 1.5 collective-permute-start.10
  197.5 4.0 %collective-permute-start.11 = (f32[72,128]{1,0:T(8,128)S(1)}, f32[72,128]{1,0:T(8,128)S(1)}, u32[]{:S(2)}, u32[]{:S(2)}) collective-permute-start(f32[72,128]{1,0:T(8,128)S(1)} %add.33), channel_id=1, source_target_pairs={{0,2},{1,3},{2,0},{3,1},{4,6},{5,7},{6,4},{7,5},{8,10},{9,11},{10,... | collective-permute-start | bytes 110600 | tf_op jit(solution)/shard_map/ppermute | solution.py:604
  201.5 4.0 %collective-permute-start.12 = (f32[72,128]{1,0:T(8,128)S(1)}, f32[72,128]{1,0:T(8,128)S(1)}, u32[]{:S(2)}, u32[]{:S(2)}) collective-permute-start(f32[72,128]{1,0:T(8,128)S(1)} %add.34), channel_id=1, source_target_pairs={{0,4},{1,5},{2,6},{3,7},{4,0},{5,1},{6,2},{7,3},{8,12},{9,13},{10,... | collective-permute-start | bytes 110600 | tf_op jit(solution)/shard_map/ppermute | solution.py:604
  205.5 4.0 %collective-permute-start.13 = (f32[72,128]{1,0:T(8,128)S(1)}, f32[72,128]{1,0:T(8,128)S(1)}, u32[]{:S(2)}, u32[]{:S(2)}) collective-permute-start(f32[72,128]{1,0:T(8,128)S(1)} %add.35), channel_id=1, source_target_pairs={{0,8},{1,9},{2,10},{3,11},{4,12},{5,13},{6,14},{7,15},{8,0},{9,1},... | collective-permute-start | bytes 110600 | tf_op jit(solution)/shard_map/ppermute | solution.py:604
  209.4 4.9 %collective-permute-start.14 = (f32[72,128]{1,0:T(8,128)S(1)}, f32[72,128]{1,0:T(8,128)S(1)}, u32[]{:S(2)}, u32[]{:S(2)}) collective-permute-start(f32[72,128]{1,0:T(8,128)S(1)} %add.36), channel_id=1, source_target_pairs={{0,16},{1,17},{2,18},{3,19},{4,20},{5,21},{6,22},{7,23},{8,24},{9,... | collective-permute-start | bytes 110600 | tf_op jit(solution)/shard_map/ppermute | solution.py:604
  215.5 1.0 copy-start.8

commit v4 on v3

--- a/solution.py
+++ b/solution.py
@@ -10,11 +10,12 @@
 
 DIM = 32
 LANES = 128
-UNROLL = 48
+UNROLL = 96
 SUMS = 3
 CHUNK = 256
 DENSE = 1024
 LINE = 1024
+VMEM_LIMIT = 65400 * 1024
 AXES = ("node", "query")
 HIGHEST = lax.Precision.HIGHEST
 SMEM = pl.BlockSpec(memory_space=pltpu.SMEM)
@@ -33,7 +34,7 @@
         half = self.nodes // 2
         low = part % half
         node = (column & 1) * half + (low ^ (low >> 1))
-        return node * self.queries + (column >> 1) * 2 + part // half
+        return node * self.queries + (column >> 1) * 2 + 1 - part // half
 
     def blocks(self):
         return [(p, c) for p in range(self.nodes) for c in range(self.queries)]
@@ -152,10 +153,8 @@
     slot = slots[...]
     quarter = sum(((slot >= k * row_count).astype(jnp.int32) for k in range(1, 4)))
     local = slot - quarter * row_count
-    kind = jnp.where(
-        quarter == 1, 0, jnp.where(quarter == 3, 1, jnp.where(quarter == 0, 2, 3))
-    )
-    second = jnp.where((kind == 1) | (kind == 3), row_count, 0)
+    kind = jnp.where((quarter == 1) | (quarter == 3), 0, 1)
+    second = jnp.where(quarter >= 2, row_count, 0)
     row_bits = (row_count - 1).bit_length()
     word[...] = (rels[...] << (2 * row_bits + 1)) | (rows[...] << (row_bits + 1)) | (second + local)
     shape = (LANES, LANES)
@@ -167,7 +166,7 @@
     ones = jnp.ones((LANES, LANES), jnp.bfloat16)
     place = jnp.zeros((lines, LANES), jnp.float32)
     begin = jnp.zeros((1, LANES), jnp.float32)
-    for k in range(4):
+    for k in range(2):
         chosen = (kind == k).astype(jnp.float32)
         onehot = chosen.astype(jnp.bfloat16)
         within = jnp.dot(onehot, upto, preferred_element_type=jnp.float32)
@@ -177,25 +176,29 @@
         place = place + chosen * (begin + before + within - 1.0)
         meta[k : k + 1, :] = (begin + count).astype(jnp.int32)
         begin = begin + jnp.floor((count + (UNROLL - 0.5)) / UNROLL) * UNROLL
-        meta[k + 4 : k + 5, :] = begin.astype(jnp.int32)
-    pos[...] = place.astype(jnp.int32)
+        meta[k + 2 : k + 3, :] = begin.astype(jnp.int32)
+    spots = place.astype(jnp.int32)
+    half = lines // 2
+    pos[...] = spots[:half] | (spots[half:] << 16)
     wait(fetch([(pos, pos_buf), (word, word_buf), (meta, meta_buf)], sems))
 
     def step(i, carry):
         for u in range(LANES):
-            out_ref[pos_buf[i, u]] = word_buf[i, u]
-        return carry
-
-    lax.fori_loop(0, lines, step, 0)
+            spot = pos_buf[i, u]
+            out_ref[spot & 0xFFFF] = word_buf[i, u]
+            out_ref[spot >> 16] = word_buf[half + i, u]
+        return carry
+
+    lax.fori_loop(0, half, step, 0)
     dummy = rel_count << (2 * row_bits + 1)
 
     def fill(i, carry):
         out_ref[i] = dummy
         return carry
 
-    for k in range(4):
-        lax.fori_loop(meta_buf[k, 0], meta_buf[k + 4, 0], fill, 0)
-        ends_ref[k] = meta_buf[k + 4, 0]
+    for k in range(2):
+        lax.fori_loop(meta_buf[k, 0], meta_buf[k + 2, 0], fill, 0)
+        ends_ref[k] = meta_buf[k + 2, 0]
 
 
 def split(values):
@@ -309,7 +312,7 @@
     states[1].wait()
     spread(mirror_buf, window, long)
     wait(lists)
-    walk(groups, 0, tail[1], source, target, rel, window, table_buf, sums)
+    walk(groups, 0, tail[0], source, target, rel, window, table_buf, sums)
     send_total(sums, out, sems.at[pl.ds(7, 4)])
 
 
@@ -328,13 +331,13 @@
     spread(own_buf, window, 0)
     advance(mirror_buf, mixed_buf, window, long, split(block_weight(weights[0])), block_bias(biases[0:1, :]))
     wait(lists)
-    walk(groups, 0, tail[1], source, target, rel, window, table_buf, sums)
+    walk(groups, 0, tail[0], source, target, rel, window, table_buf, sums)
     send_total(sums, out, sems.at[pl.ds(8, 4)])
 
 
 def add_boundary(groups, heads, head_rows, ref, long):
     for q in range(head_rows.shape[0]):
-        row = heads[4 + q]
+        row = heads[2 + q]
 
         @pl.when((row >= 0) & (row < long // groups))
         def _():
@@ -366,7 +369,7 @@
     wait(lists)
     extra = fetch([(own, own_buf)], sems.at[pl.ds(8, 1)])
     add_boundary(groups, tail, head_rows, sums[0], long)
-    walk(groups, tail[1], tail[3], source, target, rel, window, table_buf, sums)
+    walk(groups, tail[0], tail[1], source, target, rel, window, table_buf, sums)
     wait(extra)
     spread(own_buf, window, 0)
     wide = split_weight(block_weight(weights[0]))
@@ -423,7 +426,7 @@
     wait(lists)
     extra = fetch([(own, own_buf), (cotangent, cotangent_buf)], sems.at[pl.ds(10, 2)])
     add_boundary(groups, tail, head_rows, sums[0], long)
-    walk(groups, tail[1], tail[3], source, target, rel, window, table_buf, sums)
+    walk(groups, tail[0], tail[1], source, target, rel, window, table_buf, sums)
     wait(extra)
     spread(own_buf, window, 0)
     spread(cotangent_buf, window, long)
@@ -538,11 +541,11 @@
 
         lax.fori_loop(0, long // DENSE, step, 0)
 
-    walk(groups, tail[1], tail[3], target, source, rel, window, table_buf, sums)
+    walk(groups, tail[0], tail[1], target, source, rel, window, table_buf, sums)
     wait(late)
     add_products(bufs[0], bufs[1], 0, True)
     add_products(bufs[2], bufs[3], long, True)
-    walk(groups, 0, tail[1], target, source, rel, window, table_buf, sums)
+    walk(groups, 0, tail[0], target, source, rel, window, table_buf, sums)
     add_products(bufs[4], bufs[5], 0, False)
     add_products(bufs[6], bufs[7], long, False)
     out[...] = jnp.zeros_like(out)
@@ -560,20 +563,22 @@
     tile_count, _, slot_total = edge_tiles.shape
     lines = tile_count * slot_total // LANES
     row_bits = (row_count - 1).bit_length()
-    room = (tile_count * slot_total + 5 * UNROLL + LINE - 1) // LINE * LINE
+    room = (tile_count * slot_total + 3 * UNROLL + LINE - 1) // LINE * LINE
     flat = pltpu.VMEM((lines, LANES), jnp.int32)
     flat_smem = pltpu.SMEM((lines, LANES), jnp.int32)
+    packed = pltpu.VMEM((lines // 2, LANES), jnp.int32)
+    packed_smem = pltpu.SMEM((lines // 2, LANES), jnp.int32)
     words, ends = pl.pallas_call(
         functools.partial(
             bucket_kernel, tile_count=tile_count, row_count=row_count, rel_count=rel_count
         ),
         out_shape=[
-            jax.ShapeDtypeStruct((room,), jnp.int32), jax.ShapeDtypeStruct((4,), jnp.int32)
+            jax.ShapeDtypeStruct((room,), jnp.int32), jax.ShapeDtypeStruct((2,), jnp.int32)
         ],
         in_specs=[VMEM],
         out_specs=[SMEM] * 2,
-        scratch_shapes=[flat] * 5
-        + [pltpu.VMEM((8, LANES), jnp.int32), flat_smem, flat_smem]
+        scratch_shapes=[flat] * 3
+        + [packed, flat, pltpu.VMEM((8, LANES), jnp.int32), packed_smem, flat_smem]
         + [pltpu.SMEM((8, LANES), jnp.int32), pltpu.SemaphoreType.DMA((3,))],
         name="bucket",
     )(edge_tiles.transpose(1, 0, 2))
@@ -604,7 +609,10 @@
         return lax.ppermute(block, AXES, route)
 
     def run(fn, args, specs, outs, out_specs, scratch):
-        return pl.pallas_call(fn, out_shape=outs, in_specs=specs, out_specs=out_specs, scratch_shapes=scratch)(*args)
+        return pl.pallas_call(
+            fn, out_shape=outs, in_specs=specs, out_specs=out_specs, scratch_shapes=scratch,
+            compiler_params=pltpu.CompilerParams(vmem_limit_bytes=VMEM_LIMIT),
+        )(*args)
 
     wide_f32 = jax.ShapeDtypeStruct((long, LANES), jnp.float32)
     wide_bf16 = jax.ShapeDtypeStruct((long, LANES), jnp.bfloat16)
@@ -623,7 +631,7 @@
     tail_room = -(-tail.shape[0] // LINE) * LINE
     tail = jnp.pad(tail, (0, tail_room - tail.shape[0]))
     flat = send(jnp.concatenate([source, target, rel, tail]), seats.gather())
-    own_relation = flat[3 * room + 4 + query_count : 3 * room + 4 + 2 * query_count]
+    own_relation = flat[3 * room + 2 + query_count : 3 * room + 2 + 2 * query_count]
     grad_out = send(cotangent, seats.gather())
 
     choose_rel = (own_relation[:, None] == lax.iota(jnp.int32, query_table.shape[0])[None, :]).astype(

time: 223 us -> 211 us (0.946)
  starting transfers between devices: 21 us -> 10.7 us
  waiting for transfers between devices: 73.4 us -> 80.3 us
  local copies, waits for them, and re-layouts: 7.31 us -> 1.98 us
  Pallas kernels: 112 us -> 109 us
    ppermute x15, starting transfers between devices: 21 us -> 10.7 us  [send(): return lax.ppermute(block, AXES, route)]
    ppermute x15, waiting for transfers between devices: 73.4 us -> 80.3 us  [send(): return lax.ppermute(block, AXES, route)]
    unnamed x18 -> x2, local copies, waits for them, and re-layouts: 5.96 us -> 0.63 us
  transfers between devices with their start and end apart: 15 -> 15, of which waited for: 9 -> 10; matrix products, arithmetic and copies ran while one was open for 2% -> 3% of each run, Pallas kernels for 35% -> 36%
where the time goes in v4:
time: 211 us; the launch traced here: 208 us
  Pallas kernels  109 us (52%)
  waiting for transfers between devices  80.3 us (38%)
  starting transfers between devices  10.7 us (5%)
  other arithmetic  3.67 us (2%)
    pallas_call x7, Pallas kernels, run(): pl.pallas_call(fn, out_shape=outs, in_specs=specs, out_specs=out_specs, s...  92.7 us
    ppermute x15, waiting for transfers between devices, send(): return lax.ppermute(block, AXES, route)  80.3 us
    pallas_call x1, Pallas kernels, edge_lists(): pl.pallas_call(functools.partial(bucket_kernel, tile_count=tile_count, ro...  16.5 us
    ppermute x15, starting transfers between devices, send(): return lax.ppermute(block, AXES, route)  10.7 us
  transfers between devices with their start and end apart: 15, of which 10 were waited for; matrix products, arithmetic and copies ran while one was open for 3% of the time, Pallas kernels for 36%

profile of v4, /device:TPU:10, one launch (start us, length us, event | category | flops | bytes accessed | tf_op | source)
XLA Modules:
  0.0 207.8 jit_solution(7012478968176324235)
XLA Ops:
  0.7 16.5 %bucket.1 = (s32[9216]{0:T(1024)}, s32[2]{0:T(128)}) custom-call(s32[3,16,512]{2,1,0:T(8,128)} %bitcast.9), custom_call_target="tpu_custom_call" | custom-call | tf_op jit(solution)/shard_map/bucket/pallas_call | solution.py:571
  19.4 5.1 %collective-permute-done.1.own = bf16[1024,512]{1,0:T(8,128)(2,1)} collective-permute-done((bf16[1024,512]{1,0:T(8,128)(2,1)}, bf16[1024,512]{1,0:T(8,128)(2,1)}, u32[]{:S(2)}, u32[]{:S(2)}) %collective-permute-start.1) | collective-permute-done | bytes 1048608 | tf_op jit(solution)/shard_map/ppermute | solution.py:609
  24.6 1.7 collective-permute-start.4
  26.3 2.1 %collective-permute-start.3 = (bf16[1024,512]{1,0:T(8,128)(2,1)}, bf16[1024,512]{1,0:T(8,128)(2,1)}, u32[]{:S(2)}, u32[]{:S(2)}) collective-permute-start(bf16[1024,512]{1,0:T(8,128)(2,1)} %collective-permute-done.1.own), channel_id=1, source_target_pairs={{5,1},{21,17},{7,3},{23,19},{13,5},{29,21},{15,7},{31,23},{9,13},{... | collective-permute-start | bytes 3145736 | tf_op jit(solution)/shard_map/ppermute | solution.py:609
  28.5 28.0 %collective-permute-done.flat = s32[28672]{0:T(1024)S(1)} collective-permute-done((s32[28672]{0:T(1024)S(1)}, s32[28672]{0:T(1024)S(1)}, u32[]{:S(2)}, u32[]{:S(2)}) %collective-permute-start) | collective-permute-done | bytes 114720 | tf_op jit(solution)/shard_map/ppermute | solution.py:609
  57.2 1.1 fusion
  59.1 12.5 %shard_map.112.near = f32[4096,128]{1,0:T(8,128)} custom-call(f32[2,32,822]{2,1,0:T(8,128)} %bitcast.4, s32[28672]{0:T(1024)} %copy-done, bf16[1024,512]{1,0:T(8,128)(2,1)} %collective-permute-done.1.own, bf16[1024,512]{1,0:T(8,128)(2,1)} %collective-permute-done.4.mirror), custom_call_target="tpu_custom_call" | custom-call | tf_op jit(solution)/shard_map/pallas_call | solution.py:612
  71.6 13.5 %shard_map.113 = (bf16[4096,128]{1,0:T(8,128)(2,1)}, bf16[4096,128]{1,0:T(8,128)(2,1)}) custom-call(f32[2,32,822]{2,1,0:T(8,128)} %bitcast.5, f32[16,128]{1,0:T(8,128)} %compare_select_fusion.head_rows, f32[2,32,32]{2,1,0:T(8,128)} %weights.7, f32[2,32]{1,0:T(2,128)} %biases.7, s32[28672]{0:T(1024)} %copy-done, ...), custom_call_target="tpu_custom_call" | custom-call | tf_op jit(solution)/shard_map/pallas_call | solution.py:612
  85.4 2.0 collective-permute-start.5
  87.4 0.8 collective-permute-done.7.mirror_mixed.mirror.refs_6_
  88.2 13.5 %shard_map.114.near = f32[4096,128]{1,0:T(8,128)} custom-call(f32[2,32,822]{2,1,0:T(8,128)} %bitcast.6, f32[2,32,32]{2,1,0:T(8,128)} %weights.7, f32[2,32]{1,0:T(2,128)} %biases.7, s32[28672]{0:T(1024)} %copy-done, bf16[4096,128]{1,0:T(8,128)(2,1)} %get-tuple-element.20.own, bf16[1024,512]{1,0:T(8,128)(2,1)} %collective-permute-done.4.mirror, ...), custom_call_target="tpu_custom_call" | custom-call | tf_op jit(solution)/shard_map/pallas_call | solution.py:612
  101.8 16.6 %collective-permute-done.8.cotangent = bf16[1024,512]{1,0:T(8,128)(2,1)} collective-permute-done((bf16[1024,512]{1,0:T(8,128)(2,1)}, bf16[1024,512]{1,0:T(8,128)(2,1)}, u32[]{:S(2)}, u32[]{:S(2)}) %collective-permute-start.8) | collective-permute-done | bytes 1048608 | tf_op jit(solution)/shard_map/ppermute | solution.py:609
  118.4 15.8 %collective-permute-done.6.right_mixed.refs_2_ = bf16[4096,128]{1,0:T(8,128)(2,1)} collective-permute-done((bf16[4096,128]{1,0:T(8,128)(2,1)}, bf16[4096,128]{1,0:T(8,128)(2,1)}, u32[]{:S(2)}, u32[]{:S(2)}) %collective-permute-start.6) | collective-permute-done | bytes 1048608 | tf_op jit(solution)/shard_map/ppermute | solution.py:609
  134.2 19.0 %shard_map.115 = (bf16[1024,512]{1,0:T(8,128)(2,1)}, bf16[4096,128]{1,0:T(8,128)(2,1)}, f32[4096,128]{1,0:T(8,128)}, f32[4096,128]{1,0:T(8,128)}, f32[128,128]{1,0:T(8,128)}, /*index=5*/f32[1,128]{1,0:T(1,128)}) custom-call(f32[2,32,822]{2,1,0:T(8,128)} %bitcast.7, f32[16,128]{1,0:T(8,128)} %compare_select_fusion.head_rows, f32[2,32,32]{2,1,0:T(8,128)} %weights.7, ...), custom_call_target="tpu_custom_call" | custom-call | tf_op jit(solution)/shard_map/pallas_call | solution.py:612
  153.3 6.8 %shard_map.117 = (f32[4096,128]{1,0:T(8,128)}, f32[4096,128]{1,0:T(8,128)}, f32[128,128]{1,0:T(8,128)}, f32[1,128]{1,0:T(1,128)}) custom-call(f32[2,32,32]{2,1,0:T(8,128)} %weights.7, f32[2,32]{1,0:T(2,128)} %biases.7, bf16[1024,512]{1,0:T(8,128)(2,1)} %collective-permute-done.8.cotangent, bf16[4096,128]{1,0:T(8,128)(2,1)} %get-tuple-element.19.own.refs_4_, ...), custom_call_target="tpu_custom_call" | custom-call | tf_op jit(solution)/shard_map/pallas_call | solution.py:612
  160.1 25.1 %shard_map.118 = f32[72,128]{1,0:T(8,128)} custom-call(f32[2,32,822]{2,1,0:T(8,128)} %bitcast.8, f32[128,128]{1,0:T(8,128)} %get-tuple-element.22.weight_zero, f32[1,128]{1,0:T(1,128)} %get-tuple-element.23.bias_zero, f32[128,128]{1,0:T(8,128)} %get-tuple-element.24.weight_one, f32[1,128]{1,0:T(1,128)} %get-tuple-element.25.bias_one, s32[28672]{0:T(1024)} %copy-done, ...), custom_call_target="tpu_custom_call" | custom-call | tf_op jit(solution)/shard_map/pallas_call | solution.py:612
  185.8 1.1 collective-permute-done.10
  187.6 1.5 collective-permute-start.11
  189.1 2.4 %collective-permute-done.11 = f32[72,128]{1,0:T(8,128)S(1)} collective-permute-done((f32[72,128]{1,0:T(8,128)S(1)}, f32[72,128]{1,0:T(8,128)S(1)}, u32[]{:S(2)}, u32[]{:S(2)}) %collective-permute-start.11) | collective-permute-done | bytes 36896 | tf_op jit(solution)/shard_map/ppermute | solution.py:609
  191.6 1.6 collective-permute-start.12
  193.2 2.3 %collective-permute-done.12 = f32[72,128]{1,0:T(8,128)S(1)} collective-permute-done((f32[72,128]{1,0:T(8,128)S(1)}, f32[72,128]{1,0:T(8,128)S(1)}, u32[]{:S(2)}, u32[]{:S(2)}) %collective-permute-start.12) | collective-permute-done | bytes 36896 | tf_op jit(solution)/shard_map/ppermute | solution.py:609
  195.6 3.9 %collective-permute-done.13 = f32[72,128]{1,0:T(8,128)S(1)} collective-permute-done((f32[72,128]{1,0:T(8,128)S(1)}, f32[72,128]{1,0:T(8,128)S(1)}, u32[]{:S(2)}, u32[]{:S(2)}) %collective-permute-start.13) | collective-permute-done | bytes 36896 | tf_op jit(solution)/shard_map/ppermute | solution.py:609
  200.2 4.2 %collective-permute-done.14 = f32[72,128]{1,0:T(8,128)S(1)} collective-permute-done((f32[72,128]{1,0:T(8,128)S(1)}, f32[72,128]{1,0:T(8,128)S(1)}, u32[]{:S(2)}, u32[]{:S(2)}) %collective-permute-start.14) | collective-permute-done | bytes 36896 | tf_op jit(solution)/shard_map/ppermute | solution.py:609
  205.6 2.2 %shard_map.116 = bf16[1024,512]{1,0:T(8,128)(2,1)} custom-call(bf16[1024,512]{1,0:T(8,128)(2,1)} %collective-permute-done.9.source), custom_call_target="tpu_custom_call" | custom-call | tf_op jit(solution)/shard_map/pallas_call | solution.py:612
  (34 shorter events, 7.3 us)
Async XLA Ops:
  0.6 23.9 %collective-permute-start.1 = (bf16[1024,512]{1,0:T(8,128)(2,1)}, bf16[1024,512]{1,0:T(8,128)(2,1)}, u32[]{:S(2)}, u32[]{:S(2)}) collective-permute-start(bf16[1024,512]{1,0:T(8,128)(2,1)} %param.9), channel_id=1, source_target_pairs={{0,1},{1,17},{2,3},{3,19},{4,5},{5,21},{6,7},{7,23},{8,13},{9,29},... | collective-permute-start | bytes 3145736 | tf_op jit(solution)/shard_map/ppermute | solution.py:609
  24.6 34.5 %collective-permute-start.4 = (bf16[1024,512]{1,0:T(8,128)(2,1)}, bf16[1024,512]{1,0:T(8,128)(2,1)}, u32[]{:S(2)}, u32[]{:S(2)}) collective-permute-start(bf16[1024,512]{1,0:T(8,128)(2,1)} %collective-permute-done.1.own), channel_id=1, source_target_pairs={{1,0},{17,16},{3,2},{19,18},{5,4},{21,20},{7,6},{23,22},{13,12},{2... | collective-permute-start | bytes 3145736 | tf_op jit(solution)/shard_map/ppermute | solution.py:609
  26.3 45.3 %collective-permute-start.3 = (bf16[1024,512]{1,0:T(8,128)(2,1)}, bf16[1024,512]{1,0:T(8,128)(2,1)}, u32[]{:S(2)}, u32[]{:S(2)}) collective-permute-start(bf16[1024,512]{1,0:T(8,128)(2,1)} %collective-permute-done.1.own), channel_id=1, source_target_pairs={{5,1},{21,17},{7,3},{23,19},{13,5},{29,21},{15,7},{31,23},{9,13},{... | collective-permute-start | bytes 3145736 | tf_op jit(solution)/shard_map/ppermute | solution.py:609
  28.4 43.2 %collective-permute-start.2 = (bf16[1024,512]{1,0:T(8,128)(2,1)}, bf16[1024,512]{1,0:T(8,128)(2,1)}, u32[]{:S(2)}, u32[]{:S(2)}) collective-permute-start(bf16[1024,512]{1,0:T(8,128)(2,1)} %collective-permute-done.1.own), channel_id=1, source_target_pairs={{8,1},{24,17},{10,3},{26,19},{1,5},{17,21},{3,7},{19,23},{5,13},{2... | collective-permute-start | bytes 3145736 | tf_op jit(solution)/shard_map/ppermute | solution.py:609
  28.4 28.1 %collective-permute-start = (s32[28672]{0:T(1024)S(1)}, s32[28672]{0:T(1024)S(1)}, u32[]{:S(2)}, u32[]{:S(2)}) collective-permute-start(s32[28672]{0:T(1024)S(1)} %pad_add_fusion), channel_id=1, source_target_pairs={{0,1},{1,17},{2,3},{3,19},{4,5},{5,21},{6,7},{7,23},{8,13},{9,29},... | collective-permute-start | bytes 344072 | tf_op jit(solution)/shard_map/ppermute | solution.py:609
  56.5 0.6 copy-start
  85.2 3.1 %collective-permute-start.7 = (bf16[4096,128]{1,0:T(8,128)(2,1)}, bf16[4096,128]{1,0:T(8,128)(2,1)}, u32[]{:S(2)}, u32[]{:S(2)}) collective-permute-start(bf16[4096,128]{1,0:T(8,128)(2,1)} %get-tuple-element.19.own.refs_4_), channel_id=1, source_target_pairs={{1,0},{17,16},{3,2},{19,18},{5,4},{21,20},{7,6},{23,22},{13,12},{2... | collective-permute-start | bytes 3145736 | tf_op jit(solution)/shard_map/ppermute | solution.py:609
  85.3 33.1 %collective-permute-start.8 = (bf16[1024,512]{1,0:T(8,128)(2,1)}, bf16[1024,512]{1,0:T(8,128)(2,1)}, u32[]{:S(2)}, u32[]{:S(2)}) collective-permute-start(bf16[1024,512]{1,0:T(8,128)(2,1)} %param.17), channel_id=1, source_target_pairs={{0,1},{1,17},{2,3},{3,19},{4,5},{5,21},{6,7},{7,23},{8,13},{9,29},... | collective-permute-start | bytes 3145736 | tf_op jit(solution)/shard_map/ppermute | solution.py:609
  85.3 48.8 %collective-permute-start.6 = (bf16[4096,128]{1,0:T(8,128)(2,1)}, bf16[4096,128]{1,0:T(8,128)(2,1)}, u32[]{:S(2)}, u32[]{:S(2)}) collective-permute-start(bf16[4096,128]{1,0:T(8,128)(2,1)} %get-tuple-element.19.own.refs_4_), channel_id=1, source_target_pairs={{5,1},{21,17},{7,3},{23,19},{13,5},{29,21},{15,7},{31,23},{9,13},{... | collective-permute-start | bytes 3145736 | tf_op jit(solution)/shard_map/ppermute | solution.py:609
  85.4 48.8 %collective-permute-start.5 = (bf16[4096,128]{1,0:T(8,128)(2,1)}, bf16[4096,128]{1,0:T(8,128)(2,1)}, u32[]{:S(2)}, u32[]{:S(2)}) collective-permute-start(bf16[4096,128]{1,0:T(8,128)(2,1)} %get-tuple-element.19.own.refs_4_), channel_id=1, source_target_pairs={{8,1},{24,17},{10,3},{26,19},{1,5},{17,21},{3,7},{19,23},{5,13},{2... | collective-permute-start | bytes 3145736 | tf_op jit(solution)/shard_map/ppermute | solution.py:609
  153.2 52.4 %collective-permute-start.9 = (bf16[1024,512]{1,0:T(8,128)(2,1)}, bf16[1024,512]{1,0:T(8,128)(2,1)}, u32[]{:S(2)}, u32[]{:S(2)}) collective-permute-start(bf16[1024,512]{1,0:T(8,128)(2,1)} %get-tuple-element.21), channel_id=1, source_target_pairs={{1,0},{17,1},{3,2},{19,3},{5,4},{21,5},{7,6},{23,7},{13,8},{29,9},... | collective-permute-start | bytes 3145736 | tf_op jit(solution)/shard_map/ppermute | solution.py:609
  185.2 1.6 collective-permute-start.10
  187.6 4.0 %collective-permute-start.11 = (f32[72,128]{1,0:T(8,128)S(1)}, f32[72,128]{1,0:T(8,128)S(1)}, u32[]{:S(2)}, u32[]{:S(2)}) collective-permute-start(f32[72,128]{1,0:T(8,128)S(1)} %add.33), channel_id=1, source_target_pairs={{0,2},{1,3},{2,0},{3,1},{4,6},{5,7},{6,4},{7,5},{8,10},{9,11},{10,... | collective-permute-start | bytes 110600 | tf_op jit(solution)/shard_map/ppermute | solution.py:609
  191.6 4.0 %collective-permute-start.12 = (f32[72,128]{1,0:T(8,128)S(1)}, f32[72,128]{1,0:T(8,128)S(1)}, u32[]{:S(2)}, u32[]{:S(2)}) collective-permute-start(f32[72,128]{1,0:T(8,128)S(1)} %add.34), channel_id=1, source_target_pairs={{0,4},{1,5},{2,6},{3,7},{4,0},{5,1},{6,2},{7,3},{8,12},{9,13},{10,... | collective-permute-start | bytes 110600 | tf_op jit(solution)/shard_map/ppermute | solution.py:609
  195.5 4.0 %collective-permute-start.13 = (f32[72,128]{1,0:T(8,128)S(1)}, f32[72,128]{1,0:T(8,128)S(1)}, u32[]{:S(2)}, u32[]{:S(2)}) collective-permute-start(f32[72,128]{1,0:T(8,128)S(1)} %add.35), channel_id=1, source_target_pairs={{0,8},{1,9},{2,10},{3,11},{4,12},{5,13},{6,14},{7,15},{8,0},{9,1},... | collective-permute-start | bytes 110600 | tf_op jit(solution)/shard_map/ppermute | solution.py:609
  199.5 4.9 %collective-permute-start.14 = (f32[72,128]{1,0:T(8,128)S(1)}, f32[72,128]{1,0:T(8,128)S(1)}, u32[]{:S(2)}, u32[]{:S(2)}) collective-permute-start(f32[72,128]{1,0:T(8,128)S(1)} %add.36), channel_id=1, source_target_pairs={{0,16},{1,17},{2,18},{3,19},{4,20},{5,21},{6,22},{7,23},{8,24},{9,... | collective-permute-start | bytes 110600 | tf_op jit(solution)/shard_map/ppermute | solution.py:609
